TPU v7x, 32 devices: a whole 2x2x4 slice. The times are simulated.
32 devices in a mesh: dp: 8 (over z, x), mp: 4 (over y, core).
Axes of the slice: x: 2, y: 2, z: 4, core: 2. Of those that a mesh axis runs over, the one named last changes fastest.
Arguments:
- conv_in: bfloat16 [16384, 1024], P('dp'), may hold values from -6 to 6
- conv_weight: bfloat16 [1024, 512], P(None, 'mp'), may hold values from -0.1875 to 0.1875
- feature_gain: float32 [512], replicated, may hold values from 0.1 to 1.9
- proj_weight: bfloat16 [512, 1024], replicated, may hold values from -0.25 to 0.25
- block_gain: float32 [1024], replicated, may hold values from 0.1 to 1.9
- w_in: bfloat16 [1024, 4096], P(None, 'mp'), may hold values from -0.1875 to 0.1875
- w_out: bfloat16 [1024, 4096], P(None, 'mp'), may hold values from -0.09375 to 0.09375
- cotangent: bfloat16 [16384, 1024], P('dp'), may hold values from -0.0625 to 0.0625
- send_index: int32 [16384], P('dp'), may hold values from 0 to 2047, as said below
- slot_valid: int32 [16384], P('dp'), may hold values from 0 to 1, as said below
Outputs:
- grad_conv_weight: float32 [1024, 512], P('dp', 'mp')
- grad_proj_weight: float32 [512, 1024], P('dp', 'mp')
- grad_w_in: float32 [1024, 4096], P('dp', 'mp')
- grad_w_out: float32 [1024, 4096], P('dp', 'mp')
Inputs may be any that keep to these rules, and one draw needn't show every extreme that they name: `send_index`: the 2048 entries held by one index of dp are a permutation of 0 to 2047; entry e * 256 + j names the local frame sent to slot j of index e. `slot_valid`: slot j of the block from source s on index e is 1 exactly when the frame it receives lies inside the source's clips; a source's frames inside clips are its first ones, at least 512 of them, and some source has all 2048.
All inputs are finite; a program needn't handle non-finite values.
Results may differ from a plain program's by a relative error of at most 0.015.
Values may be sent and summed in bfloat16 or wider, within the bound.
A program may use at most 128 MiB of HBM per device.

v0:
```python
import functools

import jax
import jax.numpy as jnp
from jax import lax
from jax.experimental import pallas as pl
from jax.experimental.pallas import tpu as pltpu
from jax.sharding import PartitionSpec as P

EPSILON = 1e-05
SQRT_HALF = 0.7071067811865476
INV_SQRT_TWO_PI = 0.3989422804014327
VMEM_LIMIT = 48 * 1024 * 1024


def gelu_exact(values):
    return 0.5 * values * (1.0 + lax.erf(values * SQRT_HALF))


def gelu_slope(values):
    return 0.5 * (1.0 + lax.erf(values * SQRT_HALF)) + values * INV_SQRT_TWO_PI * jnp.exp(
        -0.5 * values * values
    )


def normalize(values):
    row_mean = jnp.mean(values, axis=-1, keepdims=True)
    centred = values - row_mean
    inv_std = lax.rsqrt(jnp.mean(centred * centred, axis=-1, keepdims=True) + EPSILON)
    return (centred * inv_std, inv_std)


def norm_back(upstream, normed, inv_std, gain_row):
    scaled = upstream * gain_row
    first_mean = jnp.mean(scaled, axis=-1, keepdims=True)
    second_mean = jnp.mean(scaled * normed, axis=-1, keepdims=True)
    return inv_std * (scaled - first_mean - normed * second_mean)


def contract_rows(left, right):
    return lax.dot_general(
        left, right, (((0,), (0,)), ((), ())), preferred_element_type=jnp.float32
    )


def contract_cols(left, right):
    return lax.dot_general(
        left, right, (((1,), (1,)), ((), ())), preferred_element_type=jnp.float32
    )


def scatter_sum_kernel(parts, count, *refs):
    ins, outs = refs[:count], refs[count : 2 * count]
    first_in, staged, second_in = (refs[(2 + i) * count : (3 + i) * count] for i in range(3))
    send_one, recv_one, send_two, recv_two = refs[5 * count :]
    half = parts // 2
    me = lax.axis_index("dp")
    parity = lax.rem(me, 2)
    place = me // 2
    partner = me + 1 - 2 * parity
    order = list(range(1, half)) + [0]

    barrier = pltpu.get_barrier_semaphore()
    pl.semaphore_signal(
        barrier, inc=1, device_id={"dp": partner}, device_id_type=pl.DeviceIdType.MESH
    )
    for k in range(1, half):
        peer = 2 * lax.rem(place + k, half) + parity
        pl.semaphore_signal(
            barrier, inc=1, device_id={"dp": peer}, device_id_type=pl.DeviceIdType.MESH
        )
    pl.semaphore_wait(barrier, half)

    def each_tile(rows, body):
        def step(i, carry):
            body(pl.ds(pl.multiple_of(i * 16, 16), 16), i)
            return carry

        lax.fori_loop(0, rows // 16, step, 0)

    ones, twos = {}, {}
    for k in order:
        target = lax.rem(place + k, half)
        for i in range(count):
            rows = outs[i].shape[0]
            start = pl.multiple_of((2 * target + 1 - parity) * rows, rows)
            ones[k, i] = pltpu.make_async_remote_copy(
                src_ref=ins[i].at[pl.ds(start, rows)],
                dst_ref=first_in[i].at[k],
                send_sem=send_one.at[i, k],
                recv_sem=recv_one.at[i, k],
                device_id={"dp": partner},
                device_id_type=pl.DeviceIdType.MESH,
            )
            ones[k, i].start()
    for k in order:
        target = lax.rem(place + k, half)
        for i in range(count):
            rows = outs[i].shape[0]
            base = (2 * target + parity) * rows
            ones[k, i].wait_recv()

            def add(tile, step, i=i, k=k, base=base):
                mine = ins[i][pl.ds(pl.multiple_of(base + step * 16, 16), 16), :]
                total = mine.astype(jnp.float32) + first_in[i][k, tile, :].astype(jnp.float32)
                if k:
                    staged[i][k, tile, :] = total.astype(jnp.bfloat16)
                else:
                    outs[i][tile, :] = total

            each_tile(rows, add)
            if k:
                twos[k, i] = pltpu.make_async_remote_copy(
                    src_ref=staged[i].at[k],
                    dst_ref=second_in[i].at[k],
                    send_sem=send_two.at[i, k],
                    recv_sem=recv_two.at[i, k],
                    device_id={"dp": 2 * target + parity},
                    device_id_type=pl.DeviceIdType.MESH,
                )
                twos[k, i].start()
    for i in range(count):
        for k in range(1, half):
            twos[k, i].wait_recv()

        def gather(tile, step, i=i):
            total = outs[i][tile, :]
            for k in range(1, half):
                total = total + second_in[i][k, tile, :].astype(jnp.float32)
            outs[i][tile, :] = total

        each_tile(outs[i].shape[0], gather)
    for copy in list(ones.values()) + list(twos.values()):
        copy.wait_send()


def norms_kernel(
    packed, gain_feat, weight, gain_block, feat_norm, feat_inv, feat_ln, hid_norm, hid_inv, hid_ln
):
    normed, inv = normalize(packed[...].astype(jnp.float32))
    feat_norm[...] = normed
    feat_inv[...] = inv
    scaled = (normed * gain_feat[...]).astype(jnp.bfloat16)
    feat_ln[...] = scaled
    hidden = jnp.dot(scaled, weight[...], preferred_element_type=jnp.float32)
    normed, inv = normalize(hidden)
    hid_norm[...] = normed
    hid_inv[...] = inv
    hid_ln[...] = (normed * gain_block[...]).astype(jnp.bfloat16)


def norms(packed, gain_feat, weight, gain_block):
    rows, channels = packed.shape
    width = weight.shape[1]
    step = min(256, rows)

    def by_row(size):
        return pl.BlockSpec((step, size), lambda i: (i, 0))

    def whole(*shape):
        return pl.BlockSpec(shape, lambda i: (0, 0))

    def made(size, kind):
        return jax.ShapeDtypeStruct((rows, size), kind)

    return pl.pallas_call(
        norms_kernel,
        grid=(rows // step,),
        out_shape=[
            made(channels, jnp.float32), made(1, jnp.float32), made(channels, jnp.bfloat16),
            made(width, jnp.float32), made(1, jnp.float32), made(width, jnp.bfloat16),
        ],
        in_specs=[by_row(channels), whole(1, channels), whole(channels, width), whole(1, width)],
        out_specs=[by_row(size) for size in (channels, 1, channels, width, 1, width)],
        compiler_params=pltpu.CompilerParams(vmem_limit_bytes=VMEM_LIMIT // 2),
        name="norms",
    )(packed, gain_feat[None, :], weight, gain_block[None, :])


def start_copy(src, dst, send_sem, recv_sem, axis, index):
    copy = pltpu.make_async_remote_copy(
        src_ref=src,
        dst_ref=dst,
        send_sem=send_sem,
        recv_sem=recv_sem,
        device_id={axis: index},
        device_id_type=pl.DeviceIdType.MESH,
    )
    copy.start()
    return copy


def greet(peers):
    barrier = pltpu.get_barrier_semaphore()
    for axis, index in peers:
        pl.semaphore_signal(
            barrier, inc=1, device_id={axis: index}, device_id_type=pl.DeviceIdType.MESH
        )
    pl.semaphore_wait(barrier, len(peers))


def block_of(index, size):
    return pl.ds(pl.multiple_of(index * size, size), size)


def product_sum_kernel(parts, count, *refs):
    pairs = [(refs[2 * i], refs[2 * i + 1]) for i in range(count)]
    outs = refs[2 * count : 3 * count]
    made, first_in, staged, second_in = (
        refs[(3 + i) * count : (4 + i) * count] for i in range(4)
    )
    send_one, recv_one, send_two, recv_two = refs[7 * count :]
    half = parts // 2
    d = lax.axis_index("dp")
    parity = lax.rem(d, 2)
    place = d // 2
    partner = d + 1 - 2 * parity
    order = list(range(1, half)) + [0]
    greet(
        [("dp", partner)]
        + [("dp", 2 * lax.rem(place + k, half) + parity) for k in range(1, half)]
    )

    def make(i, index):
        left, right = pairs[i]
        rows = outs[i].shape[0]
        span = block_of(index, rows)
        if rows % 128 == 0:
            piece = left[:, block_of(index, rows)]
            made[i][span, :] = contract_rows(piece, right[...]).astype(jnp.bfloat16)

    def make_all(i):
        left, right = pairs[i]

        def step(t, carry):
            made[i][block_of(t, 128), :] = contract_rows(
                left[:, block_of(t, 128)], right[...]
            ).astype(jnp.bfloat16)
            return carry

        lax.fori_loop(0, left.shape[1] // 128, step, 0)

    def first(i, k):
        rows = outs[i].shape[0]
        target = lax.rem(place + k, half)
        return pltpu.make_async_remote_copy(
            src_ref=made[i].at[block_of(2 * target + 1 - parity, rows)],
            dst_ref=first_in[i].at[k],
            send_sem=send_one.at[i, k],
            recv_sem=recv_one.at[i, k],
            device_id={"dp": partner},
            device_id_type=pl.DeviceIdType.MESH,
        )

    for i in range(count):
        whole = outs[i].shape[0] % 128 != 0
        if whole:
            make_all(i)

        def send(t, carry, i=i, whole=whole):
            k = lax.rem(t + 1, half)
            if not whole:
                make(i, 2 * lax.rem(place + k, half) + 1 - parity)
            first(i, k).start()
            return carry

        lax.fori_loop(0, half, send, 0)

        def keep(t, carry, i=i):
            make(i, 2 * t + parity)
            return carry

        if not whole:
            lax.fori_loop(0, half, keep, 0)

    def each_tile(rows, body):
        def step(t, carry):
            body(block_of(t, 16), t)
            return carry

        lax.fori_loop(0, rows // 16, step, 0)

    twos = {}
    for i in range(count):
        for k in order:
            rows = outs[i].shape[0]
            target = lax.rem(place + k, half)
            base = (2 * target + parity) * rows
            first(i, k).wait_recv()

            def add(tile, step, i=i, k=k, base=base):
                mine = made[i][pl.ds(pl.multiple_of(base + step * 16, 16), 16), :]
                total = mine.astype(jnp.float32) + first_in[i][k, tile, :].astype(jnp.float32)
                if k:
                    staged[i][k, tile, :] = total.astype(jnp.bfloat16)
                else:
                    outs[i][tile, :] = total

            each_tile(rows, add)
            if k:
                twos[i, k] = start_copy(
                    staged[i].at[k],
                    second_in[i].at[k],
                    send_two.at[i, k],
                    recv_two.at[i, k],
                    "dp",
                    2 * target + parity,
                )
    for i in range(count):
        for k in range(1, half):
            twos[i, k].wait_recv()

        def gather(tile, step, i=i):
            total = outs[i][tile, :]
            for k in range(1, half):
                total = total + second_in[i][k, tile, :].astype(jnp.float32)
            outs[i][tile, :] = total

        each_tile(outs[i].shape[0], gather)
    for i in range(count):
        for k in range(half):
            first(i, k).wait_send()
    for copy in twos.values():
        copy.wait_send()


def product_sum(pairs, collective_id):
    parts = lax.axis_size("dp")
    half = parts // 2
    count = len(pairs)
    shapes = [(left.shape[1], right.shape[1]) for left, right in pairs]
    blocks = [(rows // parts, cols) for rows, cols in shapes]
    slots = [pltpu.VMEM((half,) + block, jnp.bfloat16) for block in blocks]
    sent = sum(rows * cols * 2 for rows, cols in shapes)
    return pl.pallas_call(
        functools.partial(product_sum_kernel, parts, count),
        out_shape=[jax.ShapeDtypeStruct(block, jnp.float32) for block in blocks],
        in_specs=[pl.BlockSpec(memory_space=pltpu.VMEM)] * (2 * count),
        out_specs=[pl.BlockSpec(memory_space=pltpu.VMEM)] * count,
        scratch_shapes=[pltpu.VMEM(shape, jnp.bfloat16) for shape in shapes]
        + slots * 3
        + [pltpu.SemaphoreType.DMA((count, half))] * 4,
        compiler_params=pltpu.CompilerParams(
            collective_id=collective_id, has_side_effects=True, vmem_limit_bytes=VMEM_LIMIT
        ),
        cost_estimate=pl.CostEstimate(
            flops=sent * 4000, bytes_accessed=sent * 40, transcendentals=0
        ),
        name="product_sum",
    )(*[value for pair in pairs for value in pair])


def forward_kernel(
    parts, shards, source, packed, arrived, dp_send, dp_recv, near_send, near_recv,
    far_send, far_recv, on_send, on_recv, local
):
    rows, width = source.shape[0] // parts, source.shape[1]
    d = lax.axis_index("dp")
    m = lax.axis_index("mp")
    near = m + 1 - 2 * lax.rem(m, 2)
    fars = shards // 2
    greet(
        [("dp", lax.rem(d + o, parts)) for o in range(1, parts)]
        + [("mp", near)]
        + [("mp", lax.rem(m + 2 * j, shards)) for j in range(1, fars)]
    )
    exchanged, passed, kept = [], [], []
    spans, far_copies = [], []
    for o in range(1, parts):
        target = lax.rem(d + o, parts)
        exchanged.append(
            start_copy(
                source.at[block_of(target, rows)],
                arrived.at[block_of(d, rows)],
                dp_send.at[o],
                dp_recv.at[o],
                "dp",
                target,
            )
        )

    def hand_on(o):
        for j in range(1, fars):
            far_copies[o][j - 1].wait_recv()
            col = block_of(lax.rem(m - 2 * j + shards, shards), width)
            piece = packed.at[spans[o], col]
            passed.append(
                start_copy(piece, piece, on_send.at[o, j], on_recv.at[o, j], "mp", near)
            )

    lag = 2
    nears = []
    for o in range(parts):
        span = block_of(lax.rem(d - o + parts, parts), rows)
        spans.append(span)
        if o:
            exchanged[o - 1].wait_recv()
        block = arrived.at[span] if o else source.at[span]
        mine = packed.at[span, block_of(m, width)]
        far_copies.append(
            [
                start_copy(
                    block, mine, far_send.at[o, j], far_recv.at[o, j], "mp",
                    lax.rem(m + 2 * j, shards),
                )
                for j in range(1, fars)
            ]
        )
        nears.append(start_copy(block, mine, near_send.at[o], near_recv.at[o], "mp", near))
        keep = pltpu.make_async_copy(block, mine, local.at[o])
        keep.start()
        kept.append(keep)
        if o >= lag:
            hand_on(o - lag)
    for o in range(parts - lag, parts):
        hand_on(o)
    for copy in nears + passed:
        copy.wait_recv()
    for copy in kept:
        copy.wait()
    for copy in exchanged + nears + passed + [c for group in far_copies for c in group]:
        copy.wait_send()


def forward_exchange(source, collective_id):
    parts, shards = lax.axis_size("dp"), lax.axis_size("mp")
    rows, width = source.shape
    fars = max(shards // 2, 1)
    return pl.pallas_call(
        functools.partial(forward_kernel, parts, shards),
        out_shape=jax.ShapeDtypeStruct((rows, width * shards), source.dtype),
        in_specs=[pl.BlockSpec(memory_space=pltpu.VMEM)],
        out_specs=pl.BlockSpec(memory_space=pltpu.VMEM),
        scratch_shapes=[pltpu.VMEM((rows, width), source.dtype)]
        + [pltpu.SemaphoreType.DMA((parts,))] * 4
        + [pltpu.SemaphoreType.DMA((parts, fars))] * 4
        + [pltpu.SemaphoreType.DMA((parts,))],
        compiler_params=pltpu.CompilerParams(
            collective_id=collective_id, has_side_effects=True, vmem_limit_bytes=VMEM_LIMIT
        ),
        name="forward_exchange",
    )(source)


def backward_kernel(
    parts, shards, grad, back, middle, mp_send, mp_recv, dp_send, dp_recv, local
):
    share = grad.shape[0]
    rows, width = back.shape[0] // parts, back.shape[1]
    d = lax.axis_index("dp")
    m = lax.axis_index("mp")
    greet(
        [("dp", lax.rem(d + o, parts)) for o in range(1, parts)]
        + [("mp", lax.rem(m + o, shards)) for o in range(1, shards)]
    )
    columns = []
    for o in range(1, shards):
        peer = lax.rem(m + o, shards)
        columns.append(
            start_copy(
                grad.at[:, block_of(peer, width)],
                middle.at[block_of(m, share)],
                mp_send.at[o],
                mp_recv.at[o],
                "mp",
                peer,
            )
        )
    own_column = pltpu.make_async_copy(
        grad.at[:, block_of(m, width)], middle.at[block_of(m, share)], local.at[0]
    )
    own_column.start()

    for copy in columns:
        copy.wait_recv()
    own_column.wait()
    blocks = []
    for o in range(1, parts):
        target = lax.rem(d + o, parts)
        blocks.append(
            start_copy(
                middle.at[block_of(target, rows)],
                back.at[block_of(d, rows)],
                dp_send.at[o],
                dp_recv.at[o],
                "dp",
                target,
            )
        )
    own_block = pltpu.make_async_copy(
        middle.at[block_of(d, rows)], back.at[block_of(d, rows)], local.at[1]
    )
    own_block.start()
    for copy in blocks:
        copy.wait_recv()
    own_block.wait()
    for copy in columns + blocks:
        copy.wait_send()


def backward_exchange(grad, collective_id):
    parts, shards = lax.axis_size("dp"), lax.axis_size("mp")
    share, channels = grad.shape
    back = (share * shards, channels // shards)
    return pl.pallas_call(
        functools.partial(backward_kernel, parts, shards),
        out_shape=jax.ShapeDtypeStruct(back, grad.dtype),
        in_specs=[pl.BlockSpec(memory_space=pltpu.VMEM)],
        out_specs=pl.BlockSpec(memory_space=pltpu.VMEM),
        scratch_shapes=[pltpu.VMEM(back, grad.dtype)]
        + [pltpu.SemaphoreType.DMA((shards,))] * 2
        + [pltpu.SemaphoreType.DMA((parts,))] * 2
        + [pltpu.SemaphoreType.DMA((2,))],
        compiler_params=pltpu.CompilerParams(
            collective_id=collective_id, has_side_effects=True, vmem_limit_bytes=VMEM_LIMIT
        ),
        name="backward_exchange",
    )(grad)


def scatter_sum(terms, collective_id):
    parts = lax.axis_size("dp")
    half = parts // 2
    count = len(terms)
    blocks = [(term.shape[0] // parts, term.shape[1]) for term in terms]
    slots = [pltpu.VMEM((half,) + block, jnp.bfloat16) for block in blocks]
    sent = sum(term.size * 2 for term in terms)
    return pl.pallas_call(
        functools.partial(scatter_sum_kernel, parts, count),
        out_shape=[jax.ShapeDtypeStruct(block, jnp.float32) for block in blocks],
        in_specs=[pl.BlockSpec(memory_space=pltpu.VMEM)] * count,
        out_specs=[pl.BlockSpec(memory_space=pltpu.VMEM)] * count,
        scratch_shapes=slots * 3 + [pltpu.SemaphoreType.DMA((count, half))] * 4,
        compiler_params=pltpu.CompilerParams(
            collective_id=collective_id, has_side_effects=True, vmem_limit_bytes=VMEM_LIMIT
        ),
        cost_estimate=pl.CostEstimate(
            flops=sent * 4000, bytes_accessed=sent * 40, transcendentals=0
        ),
        name="scatter_sum",
    )(*terms)


def on_device(
    conv_in,
    conv_weight,
    feature_gain,
    proj_weight,
    block_gain,
    w_in,
    w_out,
    cotangent,
    send_index,
    slot_valid,
):
    frames = conv_in.shape[0]
    shards = lax.axis_size("mp")
    member = lax.axis_index("mp")
    pre_act = jnp.dot(conv_in, conv_weight, preferred_element_type=jnp.float32)
    features = gelu_exact(pre_act).astype(jnp.bfloat16)
    choose = (send_index[:, None] == jnp.arange(frames, dtype=send_index.dtype)).astype(jnp.bfloat16)
    outgoing = jnp.dot(choose, features, preferred_element_type=jnp.float32).astype(jnp.bfloat16)
    packed = forward_exchange(outgoing, 3)
    feat_norm, feat_inv, feat_ln, hid_norm, hid_inv, hid_ln = norms(
        packed, feature_gain, proj_weight, block_gain
    )
    upward = jnp.dot(hid_ln, w_in, preferred_element_type=jnp.float32)
    valid = slot_valid.astype(jnp.float32)[:, None]
    active = (valid * gelu_exact(upward)).astype(jnp.bfloat16)
    grad_active = valid * jnp.dot(cotangent, w_out, preferred_element_type=jnp.float32)
    grad_upward = (grad_active * gelu_slope(upward)).astype(jnp.bfloat16)
    partial_value = contract_cols(grad_upward, w_in)
    share_rows = frames // shards
    first_row = member * share_rows
    share_normed = lax.psum_scatter(
        partial_value.astype(jnp.bfloat16), "mp", scatter_dimension=0, tiled=True
    ).astype(jnp.float32)
    out_grad, in_grad = product_sum([(cotangent, active), (hid_ln, grad_upward)], 1)
    share_normed, in_grad, out_grad = lax.optimization_barrier((share_normed, in_grad, out_grad))
    share_cot = lax.dynamic_slice_in_dim(valid, first_row, share_rows, 0) * (
        lax.dynamic_slice_in_dim(cotangent, first_row, share_rows, 0).astype(jnp.float32)
    )
    share_norm = lax.dynamic_slice_in_dim(hid_norm, first_row, share_rows, 0)
    share_inv = lax.dynamic_slice_in_dim(hid_inv, first_row, share_rows, 0)
    share_grad = (share_cot + norm_back(share_normed, share_norm, share_inv, block_gain)).astype(
        jnp.bfloat16
    )
    share_feat = lax.dynamic_slice_in_dim(feat_ln, first_row, share_rows, 0)
    share_feat_norm = lax.dynamic_slice_in_dim(feat_norm, first_row, share_rows, 0)
    share_feat_inv = lax.dynamic_slice_in_dim(feat_inv, first_row, share_rows, 0)
    grad_feat_ln = contract_cols(share_grad, proj_weight)
    grad_packed = norm_back(grad_feat_ln, share_feat_norm, share_feat_inv, feature_gain).astype(
        jnp.bfloat16
    )
    proj_term = contract_rows(share_feat, share_grad)
    proj_part = lax.psum_scatter(
        proj_term.astype(jnp.bfloat16), "mp", scatter_dimension=1, tiled=True
    )
    returned = backward_exchange(grad_packed, 4)
    grad_features = contract_rows(choose, returned)
    grad_pre = (grad_features * gelu_slope(pre_act)).astype(jnp.bfloat16)
    conv_term = contract_rows(conv_in, grad_pre)
    conv_grad, proj_grad = scatter_sum([conv_term.astype(jnp.bfloat16), proj_part], 2)
    grads = (conv_grad, proj_grad, in_grad, out_grad)
    result = (grads[0], grads[1], grads[2], grads[3])
    return result


def solution(mesh):
    placed = (
        P("dp", None),
        P(None, "mp"),
        P(),
        P(),
        P(),
        P(None, "mp"),
        P(None, "mp"),
        P("dp", None),
        P("dp"),
        P("dp"),
    )
    return jax.shard_map(
        on_device,
        mesh=mesh,
        in_specs=placed,
        out_specs=(P("dp", "mp"), P("dp", "mp"), P("dp", "mp"), P("dp", "mp")),
        check_vma=False,
    )
```

profile of v0, /device:TPU:1, one launch (start us, length us, event | category | flops | bytes accessed | tf_op | source)
XLA Modules:
  0.0 213.7 jit_solution(11522430567217706543)
XLA Ops:
  7.2 0.0 copy-start
  7.2 0.0 reduce-scatter.3.cloned.1.call-start
  7.2 0.8 convert_element_type.44
  8.1 3.5 %fusion.27 = f32[2048,128]{1,0:T(8,128)S(1)} fusion(bf16[2048,1024]{1,0:T(8,128)(2,1)} %param.10, bf16[1024,128]{1,0:T(8,128)(2,1)} %param.11), kind=kOutput, calls=%fused_computation.49 | convolution fusion | flops 536870912 | bytes 5505024 | tf_op jit(solution)/shard_map/dot_general | solution.py:559
  11.6 0.0 copy-start.3
  11.6 0.0 copy-start.13
  11.6 0.0 copy-start.14
  11.6 3.1 %fusion.11.source = bf16[2048,128]{1,0:T(8,128)(2,1)S(1)} fusion(s32[2048]{0:T(1024)S(1)} %copy-done.22, f32[2048,128]{1,0:T(8,128)S(1)} %fusion.27), kind=kOutput, calls=%fused_computation.16 | convolution fusion | flops 1079508992 | bytes 1581056 | tf_op jit(solution)/shard_map/dot_general | solution.py:562
  14.8 25.0 %forward_exchange.1.packed = bf16[2048,512]{1,0:T(8,128)(2,1)S(1)} custom-call(bf16[2048,128]{1,0:T(8,128)(2,1)S(1)} %fusion.11.source), custom_call_target="tpu_custom_call" | custom-call | tf_op jit(solution)/shard_map/forward_exchange/pallas_call | solution.py:429
  39.8 7.5 %norms.1 = (f32[2048,512]{1,0:T(8,128)S(1)}, f32[2048,1]{1,0:T(8,128)S(1)}, bf16[2048,512]{1,0:T(8,128)(2,1)S(1)}, f32[2048,1024]{1,0:T(8,128)S(1)}, f32[2048,1]...) custom-call(bf16[2048,512]{1,0:T(8,128)(2,1)S(1)} %forward_exchange.1.packed, f32[1,512]{1,0:T(1,128)S(1)} %bitcast.24, ...), custom_call_target="tpu_custom_call" | custom-call | tf_op jit(solution)/shard_map/norms/pallas_call | solution.py:166
  47.2 3.2 %copy-done.2 = f32[2048,1024]{1,0:T(8,128)} copy-done((f32[2048,1024]{1,0:T(8,128)}, f32[2048,1024]{1,0:T(8,128)S(1)}, u32[]{:S(2)}) %copy-start.2) | copy-done | bytes 8388632
  50.5 2.0 copy-done.8
  52.4 1.0 copy-done.11
  53.4 0.0 copy-start.9
  53.4 0.0 copy-start.21
  53.4 7.0 %multiply_convert_fusion = (bf16[2048,1024]{1,0:T(8,128)(2,1)}, f32[2048,1024]{1,0:T(8,128)S(1)}) fusion(f32[2048]{0:T(1024)S(1)} %convert_element_type.44, bf16[2048,1024]{1,0:T(8,128)(2,1)S(1)} %get-tuple-element.19.refs_2_, bf16[1024,1024]{1,0:T(8,128)(2,1)S(1)} %copy-done), kind=kOutput, calls=%fused_computation.9 | convolution fusion | flops 4307550208 | bytes 18882560 | tf_op jit(solution)/shard_map/dot_general | solution.py:567
  60.5 8.0 %fusion.6.refs_3_ = bf16[2048,1024]{1,0:T(8,128)(2,1)S(1)} fusion(f32[2048,1024]{1,0:T(8,128)S(1)} %get-tuple-element.35, bf16[2048,1024]{1,0:T(8,128)(2,1)S(1)} %copy-done.9, bf16[1024,1024]{1,0:T(8,128)(2,1)S(1)} %copy-done.21, f32[2048]{0:T(1024)S(1)} %convert_element_type.44), kind=kOutput, calls=%fused_computation.8 | convolution fusion | flops 4318035968 | bytes 18882560 | tf_op jit(solution)/shard_map/dot_general | solution.py:570
  68.5 2.0 copy-done.23
  70.5 6.3 %convolution_convert_fusion = bf16[2048,1024]{1,0:T(8,128)(2,1)} fusion(bf16[2048,1024]{1,0:T(8,128)(2,1)S(1)} %fusion.6.refs_3_, bf16[1024,1024]{1,0:T(8,128)(2,1)S(1)} %copy-done), kind=kOutput, calls=%fused_computation.13 | convolution fusion | flops 4297064448 | bytes 10485760 | tf_op jit(solution)/shard_map/dot_general | solution.py:47
  76.8 0.0 reduce-scatter.3.cloned.1.call-update
  76.8 0.2 reduce-scatter.5.cloned.1.call-start
  77.0 0.1 dynamic-slice.3
  77.1 1.1 dynamic-slice_reduce_fusion
  78.2 0.0 copy-start.10
  78.2 2.2 %copy-done.10 = bf16[2048,1024]{1,0:T(8,128)(2,1)S(1)} copy-done((bf16[2048,1024]{1,0:T(8,128)(2,1)S(1)}, bf16[2048,1024]{1,0:T(8,128)(2,1)}, u32[]{:S(2)}) %copy-start.10) | copy-done | bytes 4194328
  80.4 63.2 %product_sum.1 = (f32[128,1024]{1,0:T(8,128)S(1)}, f32[128,1024]{1,0:T(8,128)S(1)}) custom-call(bf16[2048,1024]{1,0:T(8,128)(2,1)S(1)} %copy-done.10, bf16[2048,1024]{1,0:T(8,128)(2,1)} %get-tuple-element.34.refs_1_, bf16[2048,1024]{1,0:T(8,128)(2,1)} %copy-done.15, bf16[2048,1024]{1,0:T(8,128)(2,1)} %copy-done.23), custom_call_target="tpu_custom_call" | custom-call | flops 16777216000 | bytes 167772160 | tf_op jit(solution)/shard_map/product_sum/pallas_call | solution.py:335
  143.6 0.0 copy-start.6
  143.7 0.0 reduce-scatter.3.cloned.1.call-done
  143.7 1.8 convert_element_type.48
  145.5 2.0 multiply_reduce_fusion.1
  147.5 2.5 %add_convert_fusion = bf16[512,1024]{1,0:T(8,128)(2,1)S(1)} fusion(f32[2048,1024]{1,0:T(8,128)} %copy-done.2, s32[]{:T(128)S(6)} %select_n.2, f32[512,1024]{1,0:T(8,128)S(1)} %convert_element_type.48, f32[512]{0:T(512)S(1)} %get-tuple-element.37, f32[512]{0:T(512)S(1)} %get-tuple-element.38, f32[1024]{0:T(1024)S(1)} %copy-done.13, ...), kind=kLoop, calls=%fused_computation.17 | loop fusion | flops 4718592 | bytes 6303748 | tf_op jit(solution)/shard_map/convert_element_type | solution.py:585
  150.1 2.8 %convolution_convert_fusion.1 = bf16[512,1024]{1,0:T(8,128)(2,1)} fusion(bf16[512,1024]{1,0:T(8,128)(2,1)S(1)} %add_convert_fusion, bf16[2048,512]{1,0:T(8,128)(2,1)} %copy-done.16, s32[]{:T(128)S(6)} %select_n.2), kind=kOutput, calls=%fused_computation.21 | convolution fusion | flops 537395200 | bytes 2621444 | tf_op jit(solution)/shard_map/dot_general | solution.py:41
  152.8 0.0 reduce-scatter.5.cloned.1.call-update
  152.9 1.2 dynamic-slice_reduce_fusion.1
  154.1 2.1 fusion.26
  156.2 1.5 multiply_convert_fusion.1.grad
  157.7 24.3 %backward_exchange.1 = bf16[2048,128]{1,0:T(8,128)(2,1)S(1)} custom-call(bf16[512,512]{1,0:T(8,128)(2,1)S(1)} %multiply_convert_fusion.1.grad), custom_call_target="tpu_custom_call" | custom-call | tf_op jit(solution)/shard_map/backward_exchange/pallas_call | solution.py:505
  182.1 5.0 %fusion.10.clone.4 = bf16[2048,128]{1,0:T(8,128)(2,1)S(1)} fusion(bf16[2048,128]{1,0:T(8,128)(2,1)S(1)} %backward_exchange.1, s32[2048]{0:T(1024)S(1)} %copy-done.22, f32[2048,128]{1,0:T(8,128)S(1)} %copy-done.20), kind=kOutput, calls=%fused_computation.15.clone.clone.clone.1 | convolution fusion | flops 1080557568 | bytes 2105344 | tf_op jit(solution)/shard_map/dot_general | solution.py:41
  187.1 0.0 copy-start.1
  187.1 1.8 fusion.12.refs_0_
  188.9 0.0 copy-start.7
  188.9 0.0 reduce-scatter.5.cloned.1.call-done.refs_1_
  189.0 1.0 copy-done.17
  190.0 14.0 %scatter_sum.1 = (f32[128,128]{1,0:T(8,128)S(1)}, f32[64,256]{1,0:T(8,128)S(1)}) custom-call(bf16[1024,128]{1,0:T(8,128)(2,1)S(1)} %fusion.12.refs_0_, bf16[512,256]{1,0:T(8,128)(2,1)S(1)} %copy-done.17), custom_call_target="tpu_custom_call" | custom-call | flops 2097152000 | bytes 20971520 | tf_op jit(solution)/shard_map/scatter_sum/pallas_call | solution.py:528
  204.0 0.6 copy.24
  204.6 0.6 copy.25
  205.3 0.8 copy.26
  206.1 0.8 copy.27
  (35 shorter events, 0.1 us)
Async XLA Ops:
  7.2 46.2 %copy-start = (bf16[1024,1024]{1,0:T(8,128)(2,1)S(1)}, bf16[1024,1024]{1,0:T(8,128)(2,1)}, u32[]{:S(2)}) copy-start(bf16[1024,1024]{1,0:T(8,128)(2,1)} %param.15) | copy-start | bytes 6291460
  7.2 4.4 %copy-start.22 = (s32[2048]{0:T(1024)S(1)}, s32[2048]{0:T(1024)}, u32[]{:S(2)}) copy-start(s32[2048]{0:T(1024)} %param.18) | copy-start | bytes 24580
  7.2 136.5 %reduce-scatter.3.cloned.1.call-start = ((), (), s32[]{:S(2)}) async-start(), calls=%async_computation.2 | async-start | bytes 5242880 | tf_op jit(solution)/shard_map/reduce_scatter | solution.py:575
  11.5 3.2 %copy-start.19 = (f32[2048,128]{1,0:T(8,128)}, f32[2048,128]{1,0:T(8,128)S(1)}, u32[]{:S(2)}) copy-start(f32[2048,128]{1,0:T(8,128)S(1)} %fusion.27) | copy-start | bytes 3145732
  11.6 28.2 %copy-start.3 = (bf16[512,1024]{1,0:T(8,128)(2,1)S(1)}, bf16[512,1024]{1,0:T(8,128)(2,1)}, u32[]{:S(2)}) copy-start(bf16[512,1024]{1,0:T(8,128)(2,1)} %weight.1) | copy-start | bytes 3145732
  11.6 28.2 %copy-start.13 = (f32[1024]{0:T(1024)S(1)}, f32[1024]{0:T(1024)}, u32[]{:S(2)}) copy-start(f32[1024]{0:T(1024)} %param.14) | copy-start | bytes 12292
  11.6 28.2 %copy-start.14 = (f32[512]{0:T(512)S(1)}, f32[512]{0:T(512)}, u32[]{:S(2)}) copy-start(f32[512]{0:T(512)} %param.12) | copy-start | bytes 6148
  47.2 3.2 %copy-start.2 = (f32[2048,1024]{1,0:T(8,128)}, f32[2048,1024]{1,0:T(8,128)S(1)}, u32[]{:S(2)}) copy-start(f32[2048,1024]{1,0:T(8,128)S(1)} %get-tuple-element.23) | copy-start | bytes 25165828
  50.5 2.0 copy-start.8
  52.4 1.0 copy-start.11
  53.4 7.0 %copy-start.12 = (f32[2048,1]{1,0:T(8,128)}, f32[2048,1]{1,0:T(8,128)S(1)}, u32[]{:S(2)}) copy-start(f32[2048,1]{1,0:T(8,128)S(1)} %get-tuple-element.18) | copy-start | bytes 24580
  53.4 7.0 %copy-start.15 = (bf16[2048,1024]{1,0:T(8,128)(2,1)}, bf16[2048,1024]{1,0:T(8,128)(2,1)S(1)}, u32[]{:S(2)}) copy-start(bf16[2048,1024]{1,0:T(8,128)(2,1)S(1)} %get-tuple-element.19.refs_2_) | copy-start | bytes 12582916
  53.4 7.0 %copy-start.16 = (bf16[2048,512]{1,0:T(8,128)(2,1)}, bf16[2048,512]{1,0:T(8,128)(2,1)S(1)}, u32[]{:S(2)}) copy-start(bf16[2048,512]{1,0:T(8,128)(2,1)S(1)} %get-tuple-element.25) | copy-start | bytes 6291460
  53.4 7.0 %copy-start.9 = (bf16[2048,1024]{1,0:T(8,128)(2,1)S(1)}, bf16[2048,1024]{1,0:T(8,128)(2,1)}, u32[]{:S(2)}) copy-start(bf16[2048,1024]{1,0:T(8,128)(2,1)} %refs_0_.1) | copy-start | bytes 12582916
  53.4 7.0 %copy-start.21 = (bf16[1024,1024]{1,0:T(8,128)(2,1)S(1)}, bf16[1024,1024]{1,0:T(8,128)(2,1)}, u32[]{:S(2)}) copy-start(bf16[1024,1024]{1,0:T(8,128)(2,1)} %param.16) | copy-start | bytes 6291460
  68.5 2.0 copy-start.23
  76.8 112.2 %reduce-scatter.5.cloned.1.call-start = ((), (), s32[]{:S(2)}) async-start(), calls=%async_computation.3 | async-start | bytes 1310720 | tf_op jit(solution)/shard_map/reduce_scatter | solution.py:596
  78.2 2.2 %copy-start.10 = (bf16[2048,1024]{1,0:T(8,128)(2,1)S(1)}, bf16[2048,1024]{1,0:T(8,128)(2,1)}, u32[]{:S(2)}) copy-start(bf16[2048,1024]{1,0:T(8,128)(2,1)} %refs_0_.1) | copy-start | bytes 12582916
  143.6 6.4 %copy-start.4 = (f32[128,1024]{1,0:T(8,128)}, f32[128,1024]{1,0:T(8,128)S(1)}, u32[]{:S(2)}) copy-start(f32[128,1024]{1,0:T(8,128)S(1)} %get-tuple-element.46) | copy-start | bytes 1572868
  143.6 6.4 %copy-start.6 = (f32[128,1024]{1,0:T(8,128)}, f32[128,1024]{1,0:T(8,128)S(1)}, u32[]{:S(2)}) copy-start(f32[128,1024]{1,0:T(8,128)S(1)} %get-tuple-element.45) | copy-start | bytes 1572868
  152.9 29.2 %copy-start.20 = (f32[2048,128]{1,0:T(8,128)S(1)}, f32[2048,128]{1,0:T(8,128)}, u32[]{:S(2)}) copy-start(f32[2048,128]{1,0:T(8,128)} %copy-done.19) | copy-start | bytes 3145732
  182.1 5.0 %copy-start.18 = (bf16[2048,1024]{1,0:T(8,128)(2,1)S(1)}, bf16[2048,1024]{1,0:T(8,128)(2,1)}, u32[]{:S(2)}) copy-start(bf16[2048,1024]{1,0:T(8,128)(2,1)} %param.10) | copy-start | bytes 12582916
  187.1 19.7 %copy-start.1 = (bf16[1024,1024]{1,0:T(8,128)(2,1)S(1)}, bf16[1024,1024]{1,0:T(8,128)(2,1)}, u32[]{:S(2)}) copy-start(bf16[1024,1024]{1,0:T(8,128)(2,1)} %param.15) | copy-start | bytes 6291460
  188.9 16.4 %copy-start.7 = (f32[128,1024]{1,0:T(8,128)S(1)}, f32[128,1024]{1,0:T(8,128)}, u32[]{:S(2)}) copy-start(f32[128,1024]{1,0:T(8,128)} %copy-done.6) | copy-start | bytes 1572868
  188.9 17.1 %copy-start.5 = (f32[128,1024]{1,0:T(8,128)S(1)}, f32[128,1024]{1,0:T(8,128)}, u32[]{:S(2)}) copy-start(f32[128,1024]{1,0:T(8,128)} %copy-done.4) | copy-start | bytes 1572868
  189.0 1.0 copy-start.17
Sparse Core Ops, SparseCore 0:
  76.9 45.3 reduce-scatter.2
  153.0 29.2 reduce-scatter.4
where the time goes:
time: 216 us; the launch traced here: 214 us
  Pallas kernels  134 us (62%)
  matrix products  39.6 us (18%)
  local copies, waits for them, and re-layouts  16.6 us (8%)
  between operations  14.4 us (7%)
  other arithmetic  8.72 us (4%)
    pallas_call x1, Pallas kernels, product_sum(): pl.pallas_call(functools.partial(product_sum_kernel, parts, count), out_s...  63.2 us
    pallas_call x1, Pallas kernels, forward_exchange(): pl.pallas_call(functools.partial(forward_kernel, parts, shards), out_shap...  25 us
    pallas_call x1, Pallas kernels, backward_exchange(): pl.pallas_call(functools.partial(backward_kernel, parts, shards), out_sha...  24.3 us
    unnamed x52, local copies, waits for them, and re-layouts  14.3 us
    pallas_call x1, Pallas kernels, scatter_sum(): pl.pallas_call(functools.partial(scatter_sum_kernel, parts, count), out_s...  14 us
    dot_general x3, matrix products, contract_rows(): lax.dot_general(left, right, (((0,), (0,)), ((), ())), preferred_element_...  9.55 us
    dot_general x2, matrix products, contract_cols(): lax.dot_general(left, right, (((1,), (1,)), ((), ())), preferred_element_...  8.41 us
    dot_general x1, matrix products, on_device(): jnp.dot(cotangent, w_out, preferred_element_type=jnp.float32)  8.03 us
  transfers between devices with their start and end apart: 2, of which 0 were waited for; matrix products, arithmetic and copies ran while one was open for 6% of the time, Pallas kernels for 41%

commit v1 on v0

v1 whole, which is shorter than its diff:
```python
import functools
import types

import jax
import jax.numpy as jnp
from jax import lax
from jax.experimental import pallas as pl
from jax.experimental.pallas import tpu as pltpu
from jax.sharding import PartitionSpec as P

EPSILON = 1e-05
SQRT_HALF = 0.7071067811865476
INV_SQRT_TWO_PI = 0.3989422804014327
VMEM_LIMIT = 67043328


def gelu_exact(values):
    return 0.5 * values * (1.0 + lax.erf(values * SQRT_HALF))


def gelu_slope(values):
    return 0.5 * (1.0 + lax.erf(values * SQRT_HALF)) + values * INV_SQRT_TWO_PI * jnp.exp(
        -0.5 * values * values
    )


def normalize(values):
    row_mean = jnp.mean(values, axis=-1, keepdims=True)
    centred = values - row_mean
    inv_std = lax.rsqrt(jnp.mean(centred * centred, axis=-1, keepdims=True) + EPSILON)
    return (centred * inv_std, inv_std)


def norm_back(upstream, normed, inv_std, gain_row):
    scaled = upstream * gain_row
    first_mean = jnp.mean(scaled, axis=-1, keepdims=True)
    second_mean = jnp.mean(scaled * normed, axis=-1, keepdims=True)
    return inv_std * (scaled - first_mean - normed * second_mean)


def contract_rows(left, right):
    return lax.dot_general(
        left, right, (((0,), (0,)), ((), ())), preferred_element_type=jnp.float32
    )


def contract_cols(left, right):
    return lax.dot_general(
        left, right, (((1,), (1,)), ((), ())), preferred_element_type=jnp.float32
    )


def start_copy(src, dst, send_sem, recv_sem, axis, index):
    copy = remote(src, dst, send_sem, recv_sem, axis, index)
    copy.start()
    return copy


def remote(src, dst, send_sem, recv_sem, axis, index):
    return pltpu.make_async_remote_copy(
        src_ref=src,
        dst_ref=dst,
        send_sem=send_sem,
        recv_sem=recv_sem,
        device_id={axis: index},
        device_id_type=pl.DeviceIdType.MESH,
    )


def greet(peers):
    barrier = pltpu.get_barrier_semaphore()
    for axis, index in peers:
        pl.semaphore_signal(
            barrier, inc=1, device_id={axis: index}, device_id_type=pl.DeviceIdType.MESH
        )
    pl.semaphore_wait(barrier, len(peers))


def block_of(index, size):
    return pl.ds(pl.multiple_of(index * size, size), size)


def loop(count, body):
    def step(t, carry):
        body(t)
        return carry

    lax.fori_loop(0, count, step, 0)


def step_kernel(parts, shards, names, *refs):
    r = types.SimpleNamespace(**dict(zip(names, refs)))
    outgoing, arrived, packed = r.outgoing, r.arrived, r.packed
    frames, width = outgoing.shape
    rows = frames // parts
    share = rows // shards
    fars = shards // 2
    group_rows = fars * share
    levels = parts.bit_length() - 1
    half = parts // 2
    w_in, w_out, proj, cot = r.w_in, r.w_out, r.proj, r.cot
    spare = r.spare
    d = lax.axis_index("dp")
    m = lax.axis_index("mp")
    side = lax.rem(m, 2)
    line = m // 2
    near = m + 1 - 2 * side
    piece = side * fars + line

    def load(src, dst, k):
        copy = pltpu.make_async_copy(src, dst, r.load_sem.at[k])
        copy.start()
        return copy

    load_w_out = load(r.w_out_hbm, w_out, 0)
    load_cot = load(r.cot_hbm, cot, 1)
    load_proj = load(r.proj_hbm, proj, 2)
    load_w_in = load(r.w_in_hbm, w_in, 3)

    def owner(k):
        total = 0
        for j in range(levels):
            bit = 2**j
            total = total + bit * lax.rem(lax.rem(d // bit, 2) + lax.rem(k // bit, 2), 2)
        return total

    def mate(j):
        bit = 2**j
        return d + bit - 2 * bit * lax.rem(d // bit, 2)

    def far(j):
        return lax.rem(m + 2 * j, shards)

    greet(
        [("dp", lax.rem(d + o, parts)) for o in range(1, parts)]
        + [("mp", lax.rem(m + o, shards)) for o in range(1, shards)]
    )

    def exchange(o):
        target = lax.rem(d + o, parts)
        return remote(
            outgoing.at[block_of(target, rows)],
            arrived.at[block_of(d, rows)],
            r.dp_send.at[o],
            r.dp_recv.at[o],
            "dp",
            target,
        )

    for o in range(1, parts):
        exchange(o).start()

    def source_of(o):
        return lax.rem(d - o + parts, parts)

    def place(o):
        return packed.at[block_of(source_of(o), rows), block_of(m, width)]

    def to_far(o, j, block):
        return remote(
            block, place(o), r.far_send.at[o, j], r.far_recv.at[o, j], "mp", far(j)
        )

    def to_near(o, block):
        return remote(block, place(o), r.near_send.at[o], r.near_recv.at[o], "mp", near)

    def keep(o, block):
        return pltpu.make_async_copy(block, place(o), r.keep_sem.at[o])

    def spread(o, block):
        for j in range(1, fars):
            to_far(o, j, block).start()
        to_near(o, block).start()
        keep(o, block).start()

    def relay(o):
        exchange(o).wait_recv()
        spread(o, arrived.at[block_of(source_of(o), rows)])

    def pass_on(o, j):
        col = block_of(lax.rem(m - 2 * j + shards, shards), width)
        part = packed.at[block_of(source_of(o), rows), col]
        return remote(part, part, r.pass_send.at[o, j], r.pass_recv.at[o, j], "mp", near)

    def hand_on(o):
        for j in range(1, fars):
            to_far(o, j, arrived.at[block_of(0, rows)]).wait_recv()
            pass_on(o, j).start()

    spread(0, outgoing.at[block_of(d, rows)])

    load_w_out.wait()
    load_cot.wait()

    def grad_active(t):
        span = block_of(t, rows)
        value = jnp.dot(cot[span, :], w_out[...], preferred_element_type=jnp.float32)
        spare[span, :] = (r.valid[span, :] * value).astype(jnp.bfloat16)
        now = (t + 1) // 2

        @pl.when(lax.rem(t, 2) == 1)
        def _():
            relay(now)
            hand_on(now - 1)

    loop(parts, grad_active)
    load_proj.wait()
    load_w_in.wait()

    def sum_near(s):
        return remote(
            r.normed_part.at[pl.ds(s * rows + (1 - side) * group_rows, group_rows)],
            r.near_in.at[s],
            r.sum_near_send.at[s],
            r.sum_near_recv.at[s],
            "mp",
            near,
        )

    def sum_far(s, j):
        return remote(
            r.staged.at[s, j],
            r.far_in.at[s, j],
            r.sum_far_send.at[s, j],
            r.sum_far_recv.at[s, j],
            "mp",
            far(j),
        )

    def pair_sum(s):
        sum_near(s).wait_recv()
        for j in range(fars):
            at = lax.rem(line + j, fars) * share
            mine = r.normed_part[pl.ds(pl.multiple_of(s * rows + side * group_rows + at, share), share), :]
            theirs = r.near_in[s, pl.ds(pl.multiple_of(at, share), share), :]
            total = mine.astype(jnp.float32) + theirs.astype(jnp.float32)
            if j:
                r.staged[s, j] = total.astype(jnp.bfloat16)
                sum_far(s, j).start()
            else:
                r.own_sum[s] = total

    def forward(o):
        s = source_of(o)
        span = block_of(s, rows)

        @pl.when(o + half + 1 < parts)
        def _():
            relay(o + half + 1)

        @pl.when(o + half < parts)
        def _():
            hand_on(o + half)

        to_near(o, arrived.at[block_of(0, rows)]).wait_recv()
        for j in range(1, fars):
            pass_on(o, j).wait_recv()
        keep(o, arrived.at[block_of(0, rows)]).wait()
        normed, _ = normalize(packed[span, :].astype(jnp.float32))
        scaled = (normed * r.gain_feat[...]).astype(jnp.bfloat16)
        hidden = jnp.dot(scaled, proj[...], preferred_element_type=jnp.float32)
        normed, _ = normalize(hidden)
        r.hid_ln[span, :] = (normed * r.gain_block[...]).astype(jnp.bfloat16)
        lines = r.hid_ln[span, :]
        keep_rows = r.valid[span, :]
        units = w_in.shape[1]
        tile = min(256, units)
        for c in range(units // tile):
            cols = pl.ds(c * tile, tile)
            upward = jnp.dot(lines, w_in[:, cols], preferred_element_type=jnp.float32)
            phi = 0.5 * (1.0 + lax.erf(upward * SQRT_HALF))
            slope = phi + upward * INV_SQRT_TWO_PI * jnp.exp(-0.5 * upward * upward)
            r.active[span, cols] = (keep_rows * (upward * phi)).astype(jnp.bfloat16)
            r.grad_up[span, cols] = (spare[span, cols].astype(jnp.float32) * slope).astype(
                jnp.bfloat16
            )
        r.normed_part[span, :] = contract_cols(r.grad_up[span, :], w_in[...]).astype(
            jnp.bfloat16
        )
        sum_near(s).start()

        @pl.when(o > 0)
        def _():
            pair_sum(source_of(o - 1))

    loop(parts, forward)
    pair_sum(source_of(parts - 1))
    load_conv = load(r.conv_in_hbm, spare, 4)

    pairs = [(cot, r.active, r.out_out), (r.hid_ln, r.grad_up, r.in_out)]
    made, taken = r.made, r.taken
    big = r.out_out.shape[0]

    def halve(i, k, j):
        span = block_of(owner(k), big)
        return remote(
            made.at[i, span], taken.at[i, k], r.halve_send.at[i, k], r.halve_recv.at[i, k],
            "dp", mate(j),
        )

    def make_pair(i, first, second):
        left, right, _ = pairs[i]
        a, b = owner(first), owner(second)
        both = jnp.concatenate([left[:, block_of(a, big)], left[:, block_of(b, big)]], axis=1)
        value = contract_rows(both, right[...]).astype(jnp.bfloat16)
        made[i, block_of(a, big), :] = value[:big]
        made[i, block_of(b, big), :] = value[big:]

    def make_odd(i):
        if big % 128:
            left, right, _ = pairs[i]

            def strip(t):
                made[i, block_of(t, 128), :] = contract_rows(
                    left[:, block_of(t, 128)], right[...]
                ).astype(jnp.bfloat16)

            loop(left.shape[1] // 128, strip)

        def odd(t):
            first = parts - 1 - 2 * t
            if big % 128 == 0:
                make_pair(i, first, first - half)
            halve(i, first, 0).start()
            halve(i, first - half, 0).start()

        loop(parts // 4, odd)

    def make_even(i):
        if big % 128 == 0:
            loop(parts // 4, lambda t: make_pair(i, parts - 2 - 2 * t, half - 2 - 2 * t))

    def low_bit(k):
        return (k & -k).bit_length() - 1 if k else levels

    def settle(i, k):
        j = low_bit(k)
        out = pairs[i][2]
        base = owner(k) * big
        for low in range(j):
            halve(i, k + 2**low, low).wait_recv()

        def tile(t):
            span = pl.ds(pl.multiple_of(base + t * 16, 16), 16)
            part = pl.ds(pl.multiple_of(t * 16, 16), 16)
            total = made[i, span, :].astype(jnp.float32)
            for low in range(j):
                total = total + taken[i, k + 2**low, part, :].astype(jnp.float32)
            if k:
                made[i, span, :] = total.astype(jnp.bfloat16)
            else:
                out[part, :] = total

        loop(big // 16, tile)
        if k:
            halve(i, k, j).start()

    def at_level(j):
        return [k for k in range(parts - 1, 0, -1) if low_bit(k) == j]

    make_odd(0)

    per = min(parts, max(1, 256 // share))
    channels = packed.shape[1]

    def back_chain(g):
        sources = [g * per + i for i in range(per)]
        spans = [
            pl.ds(pl.multiple_of(s * rows + piece * share, share), share) for s in sources
        ]

        def rows_of(ref):
            return jnp.concatenate([ref[span, :] for span in spans], axis=0)

        feat_norm, feat_inv = normalize(rows_of(packed).astype(jnp.float32))
        feat_ln = (feat_norm * r.gain_feat[...]).astype(jnp.bfloat16)
        hidden = jnp.dot(feat_ln, proj[...], preferred_element_type=jnp.float32)
        hid_norm, hid_inv = normalize(hidden)
        for s in sources:
            for j in range(1, fars):
                sum_far(s, j).wait_recv()
        upstream = []
        for s in sources:
            total = r.own_sum[s]
            for j in range(1, fars):
                total = total + r.far_in[s, j].astype(jnp.float32)
            upstream.append(total)
        upstream = jnp.concatenate(upstream, axis=0)
        direct = rows_of(r.valid) * rows_of(cot).astype(jnp.float32)
        grad_hidden = (
            direct + norm_back(upstream, hid_norm, hid_inv, r.gain_block[...])
        ).astype(jnp.bfloat16)
        grad_feat = contract_cols(grad_hidden, proj[...])
        grad_packed = norm_back(grad_feat, feat_norm, feat_inv, r.gain_feat[...]).astype(
            jnp.bfloat16
        )
        for i, s in enumerate(sources):
            r.grad[s] = grad_packed[i * share : (i + 1) * share]
        term = contract_rows(feat_ln, grad_hidden)
        proj_sum = r.proj_sum

        @pl.when(g == 0)
        def _():
            proj_sum[...] = term

        @pl.when(g > 0)
        def _():
            proj_sum[...] = proj_sum[...] + term

    loop(parts // per, back_chain)

    def columns(o):
        peer = lax.rem(m + o, shards)
        return remote(
            r.grad.at[:, :, block_of(peer, width)],
            r.middle.at[:, block_of(piece, share), :],
            r.col_send.at[o],
            r.col_recv.at[o],
            "mp",
            peer,
        )

    for o in range(1, shards):
        columns(o).start()
    own_columns = pltpu.make_async_copy(
        r.grad.at[:, :, block_of(m, width)],
        r.middle.at[:, block_of(piece, share), :],
        r.own_sem.at[0],
    )
    own_columns.start()
    quarter = r.proj_out.shape[1]
    r.proj_term[...] = r.proj_sum[...].astype(jnp.bfloat16)

    def proj_columns(o):
        peer = lax.rem(m + o, shards)
        return remote(
            r.proj_term.at[:, block_of(peer, quarter)],
            r.proj_in.at[o],
            r.proj_send.at[o],
            r.proj_recv.at[o],
            "mp",
            peer,
        )

    for o in range(1, shards):
        proj_columns(o).start()

    make_even(0)
    for o in range(1, shards):
        columns(o).wait_recv()
    own_columns.wait()

    def give_back(o):
        target = lax.rem(d + o, parts)
        return remote(
            r.middle.at[target],
            r.back.at[d],
            r.back_send.at[o],
            r.back_recv.at[o],
            "dp",
            target,
        )

    for o in range(1, parts):
        give_back(o).start()
    own_block = pltpu.make_async_copy(r.middle.at[d], r.back.at[d], r.own_sem.at[1])
    own_block.start()

    make_odd(1)
    for k in at_level(1):
        settle(0, k)
    make_even(1)

    for o in range(1, shards):
        proj_columns(o).wait_recv()
    small = r.proj_out.shape[0]
    proj_total = r.proj_term[:, block_of(m, quarter)].astype(jnp.float32)
    for o in range(1, shards):
        proj_total = proj_total + r.proj_in[o].astype(jnp.float32)
    r.proj_made[...] = proj_total.astype(jnp.bfloat16)

    def direct_sum(made, taken, send, recv, size):
        def copy(o):
            target = lax.rem(d + o, parts)
            return remote(
                made.at[block_of(target, size)],
                taken.at[o],
                send.at[o],
                recv.at[o],
                "dp",
                target,
            )

        return copy

    proj_copy = direct_sum(r.proj_made, r.proj_taken, r.proj_dp_send, r.proj_dp_recv, small)
    for o in range(1, parts):
        proj_copy(o).start()
    for j in range(2, levels):
        for k in at_level(j):
            settle(0, k)

    for o in range(1, parts):
        give_back(o).wait_recv()
    own_block.wait()
    load_conv.wait()
    returned = jnp.concatenate([r.back[e] for e in range(parts)], axis=0)
    strip = min(256, frames)

    def conv_strip(t):
        span = block_of(t, strip)
        frame = t * strip + lax.broadcasted_iota(jnp.int32, (strip, frames), 0)
        chosen = jnp.where(frame == r.index_row[...], 1.0, 0.0).astype(jnp.bfloat16)
        grad_features = jnp.dot(chosen, returned, preferred_element_type=jnp.float32)
        r.grad_pre[span, :] = (grad_features * gelu_slope(r.pre_act[span, :])).astype(
            jnp.bfloat16
        )

    loop(frames // strip, conv_strip)
    conv_term = contract_rows(r.grad_pre[...], spare[...])
    r.conv_made[...] = conv_term.T.astype(jnp.bfloat16)
    mini = r.conv_out.shape[0]
    conv_copy = direct_sum(r.conv_made, r.conv_taken, r.conv_dp_send, r.conv_dp_recv, mini)
    for o in range(1, parts):
        conv_copy(o).start()

    for j in range(1, levels):
        for k in at_level(j):
            settle(1, k)
    settle(0, 0)

    def finish(copy, made, taken, out, size):
        total = made[block_of(d, size), :].astype(jnp.float32)
        for o in range(1, parts):
            copy(o).wait_recv()
            total = total + taken[o].astype(jnp.float32)
        out[...] = total

    finish(proj_copy, r.proj_made, r.proj_taken, r.proj_out, small)
    finish(conv_copy, r.conv_made, r.conv_taken, r.conv_out, mini)
    settle(1, 0)

    for o in range(1, parts):
        exchange(o).wait_send()
        give_back(o).wait_send()
        proj_copy(o).wait_send()
        conv_copy(o).wait_send()

    def drain(o):
        block = arrived.at[block_of(0, rows)]
        to_near(o, block).wait_send()
        sum_near(o).wait_send()
        for j in range(1, fars):
            to_far(o, j, block).wait_send()
            pass_on(o, j).wait_send()
            sum_far(o, j).wait_send()

    loop(parts, drain)
    for o in range(1, shards):
        columns(o).wait_send()
        proj_columns(o).wait_send()
    for i in range(2):
        for k in range(1, parts):
            halve(i, k, low_bit(k)).wait_send()


def run_step(ins, vmem_ins):
    parts, shards = lax.axis_size("dp"), lax.axis_size("mp")
    frames, width = ins["outgoing"].shape
    conv_in, proj, w_in, w_out, cot = list(ins.values())[vmem_ins:]
    rows = frames // parts
    share = rows // shards
    fars = max(shards // 2, 1)
    channels, model = proj.shape
    units = w_in.shape[1]
    taps = conv_in.shape[1]
    big, small, mini, quarter = model // parts, channels // parts, taps // parts, model // shards
    bf16, f32 = jnp.bfloat16, jnp.float32
    dma = pltpu.SemaphoreType.DMA
    outs = dict(
        conv_out=jax.ShapeDtypeStruct((mini, width), f32),
        proj_out=jax.ShapeDtypeStruct((small, quarter), f32),
        in_out=jax.ShapeDtypeStruct((big, units), f32),
        out_out=jax.ShapeDtypeStruct((big, units), f32),
    )
    scratch = dict(
        w_out=pltpu.VMEM(w_out.shape, bf16),
        cot=pltpu.VMEM(cot.shape, bf16),
        proj=pltpu.VMEM(proj.shape, bf16),
        w_in=pltpu.VMEM(w_in.shape, bf16),
        spare=pltpu.VMEM((frames, max(units, taps)), bf16),
        arrived=pltpu.VMEM((frames, width), bf16),
        packed=pltpu.VMEM((frames, channels), bf16),
        hid_ln=pltpu.VMEM((frames, model), bf16),
        active=pltpu.VMEM((frames, units), bf16),
        grad_up=pltpu.VMEM((frames, units), bf16),
        normed_part=pltpu.VMEM((frames, model), bf16),
        near_in=pltpu.VMEM((parts, fars * share, model), bf16),
        staged=pltpu.VMEM((parts, fars, share, model), bf16),
        far_in=pltpu.VMEM((parts, fars, share, model), bf16),
        own_sum=pltpu.VMEM((parts, share, model), f32),
        made=pltpu.VMEM((2, model, units), bf16),
        taken=pltpu.VMEM((2, parts, big, units), bf16),
        grad=pltpu.VMEM((parts, share, channels), bf16),
        middle=pltpu.VMEM((parts, rows, width), bf16),
        back=pltpu.VMEM((parts, rows, width), bf16),
        proj_sum=pltpu.VMEM((channels, model), f32),
        proj_term=pltpu.VMEM((channels, model), bf16),
        proj_in=pltpu.VMEM((shards, channels, quarter), bf16),
        proj_made=pltpu.VMEM((channels, quarter), bf16),
        proj_taken=pltpu.VMEM((parts, small, quarter), bf16),
        grad_pre=pltpu.VMEM((frames, width), bf16),
        conv_made=pltpu.VMEM((taps, width), bf16),
        conv_taken=pltpu.VMEM((parts, mini, width), bf16),
        load_sem=dma((5,)),
        keep_sem=dma((parts,)),
        own_sem=dma((2,)),
        dp_send=dma((parts,)),
        dp_recv=dma((parts,)),
        near_send=dma((parts,)),
        near_recv=dma((parts,)),
        sum_near_send=dma((parts,)),
        sum_near_recv=dma((parts,)),
        back_send=dma((parts,)),
        back_recv=dma((parts,)),
        proj_dp_send=dma((parts,)),
        proj_dp_recv=dma((parts,)),
        conv_dp_send=dma((parts,)),
        conv_dp_recv=dma((parts,)),
        far_send=dma((parts, fars)),
        far_recv=dma((parts, fars)),
        pass_send=dma((parts, fars)),
        pass_recv=dma((parts, fars)),
        sum_far_send=dma((parts, fars)),
        sum_far_recv=dma((parts, fars)),
        col_send=dma((shards,)),
        col_recv=dma((shards,)),
        proj_send=dma((shards,)),
        proj_recv=dma((shards,)),
        halve_send=dma((2, parts)),
        halve_recv=dma((2, parts)),
    )
    names = tuple(ins) + tuple(outs) + tuple(scratch)
    vmem = pl.BlockSpec(memory_space=pltpu.VMEM)
    anywhere = pl.BlockSpec(memory_space=pl.ANY)
    return pl.pallas_call(
        functools.partial(step_kernel, parts, shards, names),
        out_shape=list(outs.values()),
        in_specs=[vmem] * vmem_ins + [anywhere] * (len(ins) - vmem_ins),
        out_specs=[vmem] * len(outs),
        scratch_shapes=list(scratch.values()),
        compiler_params=pltpu.CompilerParams(
            collective_id=1, has_side_effects=True, vmem_limit_bytes=VMEM_LIMIT
        ),
        name="step",
    )(*ins.values())


def on_device(
    conv_in,
    conv_weight,
    feature_gain,
    proj_weight,
    block_gain,
    w_in,
    w_out,
    cotangent,
    send_index,
    slot_valid,
):
    frames = conv_in.shape[0]
    pre_act = jnp.dot(conv_in, conv_weight, preferred_element_type=jnp.float32)
    features = gelu_exact(pre_act).astype(jnp.bfloat16)
    choose = (send_index[:, None] == jnp.arange(frames, dtype=send_index.dtype)).astype(jnp.bfloat16)
    outgoing = jnp.dot(choose, features, preferred_element_type=jnp.float32).astype(jnp.bfloat16)
    valid = slot_valid.astype(jnp.float32)[:, None]
    ins = dict(
        outgoing=outgoing, pre_act=pre_act, valid=valid, index_row=send_index[None, :],
        gain_feat=feature_gain[None, :], gain_block=block_gain[None, :], conv_in_hbm=conv_in,
        proj_hbm=proj_weight, w_in_hbm=w_in, w_out_hbm=w_out, cot_hbm=cotangent,
    )
    return tuple(run_step(ins, 6))


def solution(mesh):
    placed = (
        P("dp", None),
        P(None, "mp"),
        P(),
        P(),
        P(),
        P(None, "mp"),
        P(None, "mp"),
        P("dp", None),
        P("dp"),
        P("dp"),
    )
    return jax.shard_map(
        on_device,
        mesh=mesh,
        in_specs=placed,
        out_specs=(P("dp", "mp"), P("dp", "mp"), P("dp", "mp"), P("dp", "mp")),
        check_vma=False,
    )
```

time: 216 us -> 140 us (0.65)
  matrix products: 39.6 us -> 7.43 us
  between operations: 14.4 us -> 0.67 us
  Pallas kernels: 134 us -> 122 us
  other arithmetic: 8.72 us -> 0.71 us
  local copies, waits for them, and re-layouts: 16.6 us -> 9.08 us
    dot_general x7 -> x0, matrix products: 33 us -> none  [the longest x3 9.55 us: contract_rows(): lax.dot_general(left, right, (((0,), (0,)), ((), ())), preferred_element_...]
    pallas_call x5 -> x1, Pallas kernels: 134 us -> 122 us  [run_step(): pl.pallas_call(functools.partial(step_kernel, parts, shards, names), out_...]
    unnamed x52 -> x8, local copies, waits for them, and re-layouts: 14.3 us -> 7.69 us
    convert_element_type x3 -> x0, other arithmetic: 5.84 us -> none  [the longest x1 2.52 us: on_device(): (share_cot + norm_back(share_normed, share_norm, share_inv, block_gain))....]
    dynamic_slice x2 -> x0, local copies, waits for them, and re-layouts: 2.27 us -> none  [the longest x1 1.18 us: on_device(): lax.dynamic_slice_in_dim(feat_inv, first_row, share_rows, 0)]
  transfers between devices with their start and end apart: 2 -> 0, of which waited for: 0 -> 0; matrix products, arithmetic and copies ran while one was open for 6% -> 0% of each run, Pallas kernels for 41% -> 0%
where the time goes in v1:
time: 140 us; the launch traced here: 139 us
  Pallas kernels  122 us (87%)
  local copies, waits for them, and re-layouts  9.08 us (6%)
  matrix products  7.43 us (5%)
    pallas_call x1, Pallas kernels, run_step(): pl.pallas_call(functools.partial(step_kernel, parts, shards, names), out_...  122 us
    unnamed x8, local copies, waits for them, and re-layouts  7.69 us
    dot_general x1, matrix products, on_device(): jnp.dot(choose, features, preferred_element_type=jnp.float32)  3.94 us
    dot_general x1, matrix products, on_device(): pre_act = jnp.dot(conv_in, conv_weight, preferred_element_type=jnp.float32)  3.48 us

profile of v1, /device:TPU:1, one launch (start us, length us, event | category | flops | bytes accessed | tf_op | source)
XLA Modules:
  0.0 139.4 jit_solution(9679290734743954711)
XLA Ops:
  0.6 0.0 copy-start.1
  0.6 0.7 convert_element_type.12
  1.3 1.4 %copy.14.refs_2_ = f32[2048,1]{1,0:T(8,128)} copy(f32[2048,1]{0,1:T(1,128)S(1)} %bitcast.6) | data formatting | bytes 16384 | tf_op jit(solution)/shard_map/broadcast_in_dim | solution.py:676
  2.7 3.5 %fusion.6.refs_1_ = f32[2048,128]{1,0:T(8,128)S(1)} fusion(bf16[2048,1024]{1,0:T(8,128)(2,1)} %refs_6_.1, bf16[1024,128]{1,0:T(8,128)(2,1)} %param.11), kind=kOutput, calls=%fused_computation.8 | convolution fusion | flops 536870912 | bytes 5505024 | tf_op jit(solution)/shard_map/dot_general | solution.py:672
  6.2 0.0 copy-start
  6.2 1.0 copy-done
  7.2 0.0 copy-done.1
  7.2 3.9 %fusion.2.refs_0_ = bf16[2048,128]{1,0:T(8,128)(2,1)} fusion(s32[2048]{0:T(1024)S(1)} %copy-done.1, f32[2048,128]{1,0:T(8,128)S(1)} %fusion.6.refs_1_), kind=kOutput, calls=%fused_computation.3 | convolution fusion | flops 1079508992 | bytes 1581056 | tf_op jit(solution)/shard_map/dot_general | solution.py:675
  11.2 121.5 %step.1 = (f32[128,128]{1,0:T(8,128)}, f32[64,256]{1,0:T(8,128)}, f32[128,1024]{1,0:T(8,128)}, f32[128,1024]{1,0:T(8,128)}) custom-call(bf16[2048,128]{1,0:T(8,128)(2,1)} %fusion.2.refs_0_, f32[2048,128]{1,0:T(8,128)} %copy-done, f32[2048,1]{1,0:T(8,128)} %copy.14.refs_2_, s32[1,2048]{1,0:T(1,128)} %bitcast.7, f32[1,512]{1,0:T(1,128)} %bitcast.9, ...), custom_call_target="tpu_custom_call" | custom-call | tf_op jit(solution)/shard_map/step/pallas_call | solution.py:646
  132.7 1.5 %copy.19 = f32[128,128]{1,0:T(8,128)} copy(f32[128,128]{1,0:T(8,128)} %get-tuple-element.8) | data formatting | bytes 131072
  134.2 1.5 %copy.20 = f32[64,256]{1,0:T(8,128)} copy(f32[64,256]{1,0:T(8,128)} %get-tuple-element.9) | data formatting | bytes 131072
  135.6 1.9 %copy.21 = f32[128,1024]{1,0:T(8,128)} copy(f32[128,1024]{1,0:T(8,128)} %get-tuple-element.10) | data formatting | bytes 1048576
  137.5 1.9 %copy.22 = f32[128,1024]{1,0:T(8,128)} copy(f32[128,1024]{1,0:T(8,128)} %get-tuple-element.11) | data formatting | bytes 1048576
Async XLA Ops:
  0.6 6.6 %copy-start.1 = (s32[2048]{0:T(1024)S(1)}, s32[2048]{0:T(1024)}, u32[]{:S(2)}) copy-start(s32[2048]{0:T(1024)} %param.18) | copy-start | bytes 24580
  6.2 1.0 copy-start

commit v2 on v1

--- a/solution.py
+++ b/solution.py
@@ -73,7 +73,7 @@
         pl.semaphore_signal(
             barrier, inc=1, device_id={axis: index}, device_id_type=pl.DeviceIdType.MESH
         )
-    pl.semaphore_wait(barrier, len(peers))
+    return barrier, len(peers)
 
 
 def block_of(index, size):
@@ -112,29 +112,45 @@
         copy.start()
         return copy
 
+    first_frames = r.normed_part
+    strips = 4
+    strip = frames // strips
+    load_weight = load(r.conv_weight_hbm, r.conv_weight, 5)
+    load_frames = [
+        load(r.conv_in_hbm.at[block_of(t, strip)], first_frames.at[block_of(t, strip)], 6 + t)
+        for t in range(strips)
+    ]
     load_w_out = load(r.w_out_hbm, w_out, 0)
     load_cot = load(r.cot_hbm, cot, 1)
     load_proj = load(r.proj_hbm, proj, 2)
     load_w_in = load(r.w_in_hbm, w_in, 3)
 
-    def owner(k):
+    def flip(index, bit):
+        return index + bit - 2 * bit * lax.rem(index // bit, 2)
+
+    def owner(bits, k):
         total = 0
-        for j in range(levels):
-            bit = 2**j
-            total = total + bit * lax.rem(lax.rem(d // bit, 2) + lax.rem(k // bit, 2), 2)
+        for j, bit in enumerate(bits):
+            total = total + bit * lax.rem(lax.rem(d // bit, 2) + lax.rem(k // 2**j, 2), 2)
         return total
-
-    def mate(j):
-        bit = 2**j
-        return d + bit - 2 * bit * lax.rem(d // bit, 2)
 
     def far(j):
         return lax.rem(m + 2 * j, shards)
 
-    greet(
+    peers = greet(
         [("dp", lax.rem(d + o, parts)) for o in range(1, parts)]
         + [("mp", lax.rem(m + o, shards)) for o in range(1, shards)]
     )
+    r.valid[...] = jnp.broadcast_to(r.valid_row[...].astype(jnp.float32), (8, frames)).T[:, :1]
+
+    load_weight.wait()
+    weight_rows = r.conv_weight[...].T
+    for t in range(strips):
+        load_frames[t].wait()
+        span = pl.ds(t * strip, strip)
+        value = contract_cols(weight_rows, first_frames[span, :])
+        r.pre_act[:, span] = value
+        r.features[:, span] = gelu_exact(value).astype(jnp.bfloat16)
 
     def exchange(o):
         target = lax.rem(d + o, parts)
@@ -147,8 +163,30 @@
             target,
         )
 
-    for o in range(1, parts):
-        exchange(o).start()
+    def pack(t, size):
+        frame = lax.broadcasted_iota(jnp.int32, (frames, size), 0)
+        chosen = jnp.where(frame == r.index_row[:, block_of(t, size)], 1.0, 0.0)
+        value = jnp.dot(
+            r.features[...], chosen.astype(jnp.bfloat16), preferred_element_type=jnp.float32
+        )
+        outgoing[block_of(t, size), :] = value.T.astype(jnp.bfloat16)
+
+    if rows % 128 == 0:
+        pl.semaphore_wait(*peers)
+
+        def pack_and_send(t):
+            pack(lax.rem(d + t + 1, parts), rows)
+
+            @pl.when(t < parts - 1)
+            def _():
+                exchange(t + 1).start()
+
+        loop(parts, pack_and_send)
+    else:
+        loop(frames // 128, lambda t: pack(t, 128))
+        pl.semaphore_wait(*peers)
+        for o in range(1, parts):
+            exchange(o).start()
 
     def source_of(o):
         return lax.rem(d - o + parts, parts)
@@ -196,9 +234,9 @@
         span = block_of(t, rows)
         value = jnp.dot(cot[span, :], w_out[...], preferred_element_type=jnp.float32)
         spare[span, :] = (r.valid[span, :] * value).astype(jnp.bfloat16)
-        now = (t + 1) // 2
-
-        @pl.when(lax.rem(t, 2) == 1)
+        now = t // 2
+
+        @pl.when((lax.rem(t, 2) == 1) & (t > 1))
         def _():
             relay(now)
             hand_on(now - 1)
@@ -244,13 +282,13 @@
         s = source_of(o)
         span = block_of(s, rows)
 
-        @pl.when(o + half + 1 < parts)
-        def _():
-            relay(o + half + 1)
-
         @pl.when(o + half < parts)
         def _():
-            hand_on(o + half)
+            relay(o + half)
+
+        @pl.when(o + half - 1 < parts)
+        def _():
+            hand_on(o + half - 1)
 
         to_near(o, arrived.at[block_of(0, rows)]).wait_recv()
         for j in range(1, fars):
@@ -287,78 +325,108 @@
     pair_sum(source_of(parts - 1))
     load_conv = load(r.conv_in_hbm, spare, 4)
 
-    pairs = [(cot, r.active, r.out_out), (r.hid_ln, r.grad_up, r.in_out)]
-    made, taken = r.made, r.taken
-    big = r.out_out.shape[0]
-
-    def halve(i, k, j):
-        span = block_of(owner(k), big)
+    natural = [2**j for j in range(levels)]
+    swapped = natural[1::-1] + natural[2:]
+    turned = natural[1:] + natural[:1]
+    big, units = r.out_out.shape
+    part = units // 2
+
+    def unit(made, taken, out, bits, send, recv):
+        return types.SimpleNamespace(
+            made=made, taken=taken, out=out, bits=bits, send=send, recv=recv, size=out.shape[0]
+        )
+
+    def big_unit(u, out, bits):
+        return unit(
+            r.made.at[u], r.taken.at[u], out.at[:, pl.ds(u % 2 * part, part)], bits,
+            r.halve_send.at[u], r.halve_recv.at[u],
+        )
+
+    out_a = big_unit(0, r.out_out, natural)
+    out_b = big_unit(1, r.out_out, swapped)
+    in_a = big_unit(2, r.in_out, natural)
+    in_b = big_unit(3, r.in_out, natural)
+    sides = [(cot, r.active, 0), (cot, r.active, 1), (r.hid_ln, r.grad_up, 0), (r.hid_ln, r.grad_up, 1)]
+    bigs = [out_a, out_b, in_a, in_b]
+    proj_unit = unit(r.proj_made, r.proj_taken, r.proj_out, turned, r.proj_dp_send, r.proj_dp_recv)
+    conv_unit = unit(r.conv_made, r.conv_taken, r.conv_out, turned, r.conv_dp_send, r.conv_dp_recv)
+
+    def halve(x, k, j):
         return remote(
-            made.at[i, span], taken.at[i, k], r.halve_send.at[i, k], r.halve_recv.at[i, k],
-            "dp", mate(j),
-        )
-
-    def make_pair(i, first, second):
-        left, right, _ = pairs[i]
-        a, b = owner(first), owner(second)
+            x.made.at[block_of(owner(x.bits, k), x.size)], x.taken.at[k], x.send.at[k],
+            x.recv.at[k], "dp", flip(d, x.bits[j]),
+        )
+
+    def make_pair(u, first, second):
+        left, right, h = sides[u]
+        x = bigs[u]
+        a, b = owner(x.bits, first), owner(x.bits, second)
         both = jnp.concatenate([left[:, block_of(a, big)], left[:, block_of(b, big)]], axis=1)
-        value = contract_rows(both, right[...]).astype(jnp.bfloat16)
-        made[i, block_of(a, big), :] = value[:big]
-        made[i, block_of(b, big), :] = value[big:]
-
-    def make_odd(i):
+        value = contract_rows(both, right[:, pl.ds(h * part, part)]).astype(jnp.bfloat16)
+        x.made[block_of(a, big), :] = value[:big]
+        x.made[block_of(b, big), :] = value[big:]
+
+    def make_odd(u):
+        x = bigs[u]
         if big % 128:
-            left, right, _ = pairs[i]
-
-            def strip(t):
-                made[i, block_of(t, 128), :] = contract_rows(
-                    left[:, block_of(t, 128)], right[...]
+            left, right, h = sides[u]
+
+            def rows_strip(t):
+                x.made[block_of(t, 128), :] = contract_rows(
+                    left[:, block_of(t, 128)], right[:, pl.ds(h * part, part)]
                 ).astype(jnp.bfloat16)
 
-            loop(left.shape[1] // 128, strip)
+            loop(left.shape[1] // 128, rows_strip)
 
         def odd(t):
             first = parts - 1 - 2 * t
             if big % 128 == 0:
-                make_pair(i, first, first - half)
-            halve(i, first, 0).start()
-            halve(i, first - half, 0).start()
+                make_pair(u, first, first - half)
+            halve(x, first, 0).start()
+            halve(x, first - half, 0).start()
 
         loop(parts // 4, odd)
 
-    def make_even(i):
+    def make_even(u):
         if big % 128 == 0:
-            loop(parts // 4, lambda t: make_pair(i, parts - 2 - 2 * t, half - 2 - 2 * t))
+            loop(parts // 4, lambda t: make_pair(u, parts - 2 - 2 * t, half - 2 - 2 * t))
 
     def low_bit(k):
         return (k & -k).bit_length() - 1 if k else levels
 
-    def settle(i, k):
+    def settle(x, k):
         j = low_bit(k)
-        out = pairs[i][2]
-        base = owner(k) * big
+        base = owner(x.bits, k) * x.size
         for low in range(j):
-            halve(i, k + 2**low, low).wait_recv()
+            halve(x, k + 2**low, low).wait_recv()
 
         def tile(t):
             span = pl.ds(pl.multiple_of(base + t * 16, 16), 16)
-            part = pl.ds(pl.multiple_of(t * 16, 16), 16)
-            total = made[i, span, :].astype(jnp.float32)
+            rows_in = pl.ds(pl.multiple_of(t * 16, 16), 16)
+            total = x.made[span, :].astype(jnp.float32)
             for low in range(j):
-                total = total + taken[i, k + 2**low, part, :].astype(jnp.float32)
+                total = total + x.taken[k + 2**low, rows_in, :].astype(jnp.float32)
             if k:
-                made[i, span, :] = total.astype(jnp.bfloat16)
+                x.made[span, :] = total.astype(jnp.bfloat16)
             else:
-                out[part, :] = total
-
-        loop(big // 16, tile)
+                x.out[rows_in, :] = total
+
+        loop(x.size // 16, tile)
         if k:
-            halve(i, k, j).start()
-
-    def at_level(j):
-        return [k for k in range(parts - 1, 0, -1) if low_bit(k) == j]
+            halve(x, k, j).start()
+
+    def settle_level(x, j):
+        for k in range(parts - 1, 0, -1):
+            if low_bit(k) == j:
+                settle(x, k)
+
+    def send_first(x):
+        for k in range(parts - 1, 0, -2):
+            halve(x, k, 0).start()
 
     make_odd(0)
+    make_odd(1)
+    make_odd(2)
 
     per = min(parts, max(1, 256 // share))
     channels = packed.shape[1]
@@ -446,6 +514,7 @@
         proj_columns(o).start()
 
     make_even(0)
+    make_even(1)
     for o in range(1, shards):
         columns(o).wait_recv()
     own_columns.wait()
@@ -466,85 +535,63 @@
     own_block = pltpu.make_async_copy(r.middle.at[d], r.back.at[d], r.own_sem.at[1])
     own_block.start()
 
-    make_odd(1)
-    for k in at_level(1):
-        settle(0, k)
-    make_even(1)
+    settle_level(out_a, 1)
+    settle_level(out_b, 1)
+    make_odd(3)
+    make_even(2)
+    make_even(3)
 
     for o in range(1, shards):
         proj_columns(o).wait_recv()
-    small = r.proj_out.shape[0]
     proj_total = r.proj_term[:, block_of(m, quarter)].astype(jnp.float32)
     for o in range(1, shards):
         proj_total = proj_total + r.proj_in[o].astype(jnp.float32)
     r.proj_made[...] = proj_total.astype(jnp.bfloat16)
 
-    def direct_sum(made, taken, send, recv, size):
-        def copy(o):
-            target = lax.rem(d + o, parts)
-            return remote(
-                made.at[block_of(target, size)],
-                taken.at[o],
-                send.at[o],
-                recv.at[o],
-                "dp",
-                target,
-            )
-
-        return copy
-
-    proj_copy = direct_sum(r.proj_made, r.proj_taken, r.proj_dp_send, r.proj_dp_recv, small)
-    for o in range(1, parts):
-        proj_copy(o).start()
+    send_first(proj_unit)
     for j in range(2, levels):
-        for k in at_level(j):
-            settle(0, k)
+        settle_level(out_a, j)
+        settle_level(out_b, j)
 
     for o in range(1, parts):
         give_back(o).wait_recv()
     own_block.wait()
     load_conv.wait()
-    returned = jnp.concatenate([r.back[e] for e in range(parts)], axis=0)
-    strip = min(256, frames)
-
-    def conv_strip(t):
-        span = block_of(t, strip)
-        frame = t * strip + lax.broadcasted_iota(jnp.int32, (strip, frames), 0)
+    returned = jnp.concatenate([r.back[e] for e in range(parts)], axis=0).T
+    tile = min(256, frames)
+
+    def conv_back(t):
+        span = block_of(t, tile)
+        frame = t * tile + lax.broadcasted_iota(jnp.int32, (tile, frames), 0)
         chosen = jnp.where(frame == r.index_row[...], 1.0, 0.0).astype(jnp.bfloat16)
-        grad_features = jnp.dot(chosen, returned, preferred_element_type=jnp.float32)
-        r.grad_pre[span, :] = (grad_features * gelu_slope(r.pre_act[span, :])).astype(
-            jnp.bfloat16
-        )
-
-    loop(frames // strip, conv_strip)
-    conv_term = contract_rows(r.grad_pre[...], spare[...])
+        grad_features = contract_cols(returned, chosen)
+        r.grad_pre[:, span] = (grad_features * gelu_slope(r.pre_act[:, span])).astype(jnp.bfloat16)
+
+    loop(frames // tile, conv_back)
+    conv_term = jnp.dot(r.grad_pre[...], spare[...], preferred_element_type=jnp.float32)
     r.conv_made[...] = conv_term.T.astype(jnp.bfloat16)
-    mini = r.conv_out.shape[0]
-    conv_copy = direct_sum(r.conv_made, r.conv_taken, r.conv_dp_send, r.conv_dp_recv, mini)
-    for o in range(1, parts):
-        conv_copy(o).start()
-
-    for j in range(1, levels):
-        for k in at_level(j):
-            settle(1, k)
-    settle(0, 0)
-
-    def finish(copy, made, taken, out, size):
-        total = made[block_of(d, size), :].astype(jnp.float32)
-        for o in range(1, parts):
-            copy(o).wait_recv()
-            total = total + taken[o].astype(jnp.float32)
-        out[...] = total
-
-    finish(proj_copy, r.proj_made, r.proj_taken, r.proj_out, small)
-    finish(conv_copy, r.conv_made, r.conv_taken, r.conv_out, mini)
-    settle(1, 0)
+    send_first(conv_unit)
+
+    settle_level(proj_unit, 1)
+    settle_level(in_a, 1)
+    settle_level(conv_unit, 1)
+    settle(out_a, 0)
+    settle(out_b, 0)
+    for j in range(2, levels):
+        settle_level(proj_unit, j)
+        settle_level(conv_unit, j)
+    settle_level(in_b, 1)
+    for j in range(2, levels):
+        settle_level(in_a, j)
+        settle_level(in_b, j)
+    settle(proj_unit, 0)
+    settle(conv_unit, 0)
+    settle(in_a, 0)
+    settle(in_b, 0)
 
     for o in range(1, parts):
         exchange(o).wait_send()
         give_back(o).wait_send()
-        proj_copy(o).wait_send()
-        conv_copy(o).wait_send()
 
     def drain(o):
         block = arrived.at[block_of(0, rows)]
@@ -559,15 +606,15 @@
     for o in range(1, shards):
         columns(o).wait_send()
         proj_columns(o).wait_send()
-    for i in range(2):
+    for x in bigs + [proj_unit, conv_unit]:
         for k in range(1, parts):
-            halve(i, k, low_bit(k)).wait_send()
+            halve(x, k, low_bit(k)).wait_send()
 
 
 def run_step(ins, vmem_ins):
     parts, shards = lax.axis_size("dp"), lax.axis_size("mp")
-    frames, width = ins["outgoing"].shape
-    conv_in, proj, w_in, w_out, cot = list(ins.values())[vmem_ins:]
+    conv_in, conv_weight, proj, w_in, w_out, cot = list(ins.values())[vmem_ins:]
+    frames, width = conv_in.shape[0], conv_weight.shape[1]
     rows = frames // parts
     share = rows // shards
     fars = max(shards // 2, 1)
@@ -589,6 +636,11 @@
         proj=pltpu.VMEM(proj.shape, bf16),
         w_in=pltpu.VMEM(w_in.shape, bf16),
         spare=pltpu.VMEM((frames, max(units, taps)), bf16),
+        conv_weight=pltpu.VMEM(conv_weight.shape, bf16),
+        valid=pltpu.VMEM((frames, 1), f32),
+        pre_act=pltpu.VMEM((width, frames), f32),
+        features=pltpu.VMEM((width, frames), bf16),
+        outgoing=pltpu.VMEM((frames, width), bf16),
         arrived=pltpu.VMEM((frames, width), bf16),
         packed=pltpu.VMEM((frames, channels), bf16),
         hid_ln=pltpu.VMEM((frames, model), bf16),
@@ -599,8 +651,8 @@
         staged=pltpu.VMEM((parts, fars, share, model), bf16),
         far_in=pltpu.VMEM((parts, fars, share, model), bf16),
         own_sum=pltpu.VMEM((parts, share, model), f32),
-        made=pltpu.VMEM((2, model, units), bf16),
-        taken=pltpu.VMEM((2, parts, big, units), bf16),
+        made=pltpu.VMEM((4, model, units // 2), bf16),
+        taken=pltpu.VMEM((4, parts, big, units // 2), bf16),
         grad=pltpu.VMEM((parts, share, channels), bf16),
         middle=pltpu.VMEM((parts, rows, width), bf16),
         back=pltpu.VMEM((parts, rows, width), bf16),
@@ -609,10 +661,10 @@
         proj_in=pltpu.VMEM((shards, channels, quarter), bf16),
         proj_made=pltpu.VMEM((channels, quarter), bf16),
         proj_taken=pltpu.VMEM((parts, small, quarter), bf16),
-        grad_pre=pltpu.VMEM((frames, width), bf16),
+        grad_pre=pltpu.VMEM((width, frames), bf16),
         conv_made=pltpu.VMEM((taps, width), bf16),
         conv_taken=pltpu.VMEM((parts, mini, width), bf16),
-        load_sem=dma((5,)),
+        load_sem=dma((10,)),
         keep_sem=dma((parts,)),
         own_sem=dma((2,)),
         dp_send=dma((parts,)),
@@ -637,8 +689,8 @@
         col_recv=dma((shards,)),
         proj_send=dma((shards,)),
         proj_recv=dma((shards,)),
-        halve_send=dma((2, parts)),
-        halve_recv=dma((2, parts)),
+        halve_send=dma((4, parts)),
+        halve_recv=dma((4, parts)),
     )
     names = tuple(ins) + tuple(outs) + tuple(scratch)
     vmem = pl.BlockSpec(memory_space=pltpu.VMEM)
@@ -656,6 +708,19 @@
     )(*ins.values())
 
 
+def hand_over_kernel(count, *refs):
+    for i in range(count):
+        refs[count + i][...] = refs[i][...]
+
+
+def hand_over(results):
+    return pl.pallas_call(
+        functools.partial(hand_over_kernel, len(results)),
+        out_shape=[jax.ShapeDtypeStruct(value.shape, value.dtype) for value in results],
+        name="hand_over",
+    )(*results)
+
+
 def on_device(
     conv_in,
     conv_weight,
@@ -668,18 +733,13 @@
     send_index,
     slot_valid,
 ):
-    frames = conv_in.shape[0]
-    pre_act = jnp.dot(conv_in, conv_weight, preferred_element_type=jnp.float32)
-    features = gelu_exact(pre_act).astype(jnp.bfloat16)
-    choose = (send_index[:, None] == jnp.arange(frames, dtype=send_index.dtype)).astype(jnp.bfloat16)
-    outgoing = jnp.dot(choose, features, preferred_element_type=jnp.float32).astype(jnp.bfloat16)
-    valid = slot_valid.astype(jnp.float32)[:, None]
     ins = dict(
-        outgoing=outgoing, pre_act=pre_act, valid=valid, index_row=send_index[None, :],
+        valid_row=slot_valid[None, :], index_row=send_index[None, :],
         gain_feat=feature_gain[None, :], gain_block=block_gain[None, :], conv_in_hbm=conv_in,
-        proj_hbm=proj_weight, w_in_hbm=w_in, w_out_hbm=w_out, cot_hbm=cotangent,
-    )
-    return tuple(run_step(ins, 6))
+        conv_weight_hbm=conv_weight, proj_hbm=proj_weight, w_in_hbm=w_in, w_out_hbm=w_out,
+        cot_hbm=cotangent,
+    )
+    return tuple(hand_over(run_step(ins, 4)))
 
 
 def solution(mesh):

time: 140 us -> 122 us (0.87)
  local copies, waits for them, and re-layouts: 9.08 us -> 0 us
  matrix products: 7.43 us -> 0 us
    unnamed x8 -> x0, local copies, waits for them, and re-layouts: 7.69 us -> none
    dot_general x2 -> x0, matrix products: 7.43 us -> none  [the longest x1 3.94 us: on_device(): jnp.dot(choose, features, preferred_element_type=jnp.float32)]
    pallas_call x1, Pallas kernels: 122 us -> 119 us  [run_step(): pl.pallas_call(functools.partial(step_kernel, parts, shards, names), out_...]
    pallas_call x0 -> x1, Pallas kernels: none -> 2.29 us  [hand_over(): pl.pallas_call(functools.partial(hand_over_kernel, len(results)), out_sha...]
where the time goes in v2:
time: 122 us
  Pallas kernels  121 us (99%)
    pallas_call x1, Pallas kernels, run_step(): pl.pallas_call(functools.partial(step_kernel, parts, shards, names), out_...  119 us

profile of v2, /device:TPU:1, one launch (start us, length us, event | category | flops | bytes accessed | tf_op | source)
XLA Modules:
  0.0 121.8 jit_solution(6428262588354507233)
XLA Ops:
  0.6 118.9 %step.1 = (f32[128,128]{1,0:T(8,128)}, f32[64,256]{1,0:T(8,128)}, f32[128,1024]{1,0:T(8,128)}, f32[128,1024]{1,0:T(8,128)}) custom-call(s32[1,2048]{1,0:T(1,128)} %bitcast.4, s32[1,2048]{1,0:T(1,128)} %bitcast.5, f32[1,512]{1,0:T(1,128)} %bitcast.7, f32[1,1024]{1,0:T(1,128)} %bitcast.6, bf16[2048,1024]{1,0:T(8,128)(2,1)} %refs_4_.1, ...), custom_call_target="tpu_custom_call" | custom-call | tf_op jit(solution)/shard_map/step/pallas_call | solution.py:698
  119.5 2.3 %hand_over.1 = (f32[128,128]{1,0:T(8,128)}, f32[64,256]{1,0:T(8,128)}, f32[128,1024]{1,0:T(8,128)}, f32[128,1024]{1,0:T(8,128)}) custom-call(f32[128,128]{1,0:T(8,128)} %get-tuple-element.8.refs_0_, f32[64,256]{1,0:T(8,128)} %get-tuple-element.9.refs_1_, f32[128,1024]{1,0:T(8,128)} %get-tuple-element.10.refs_2_, f32[128,1024]{1,0:T(8,128)} %get-tuple-element.11.refs_3_), custom_call_target="tpu_custom_call" | custom-call | tf_op jit(solution)/shard_map/hand_over/pallas_call | solution.py:717

commit v3 on v2

--- a/solution.py
+++ b/solution.py
@@ -327,7 +327,6 @@
 
     natural = [2**j for j in range(levels)]
     swapped = natural[1::-1] + natural[2:]
-    turned = natural[1:] + natural[:1]
     big, units = r.out_out.shape
     part = units // 2
 
@@ -348,8 +347,8 @@
     in_b = big_unit(3, r.in_out, natural)
     sides = [(cot, r.active, 0), (cot, r.active, 1), (r.hid_ln, r.grad_up, 0), (r.hid_ln, r.grad_up, 1)]
     bigs = [out_a, out_b, in_a, in_b]
-    proj_unit = unit(r.proj_made, r.proj_taken, r.proj_out, turned, r.proj_dp_send, r.proj_dp_recv)
-    conv_unit = unit(r.conv_made, r.conv_taken, r.conv_out, turned, r.conv_dp_send, r.conv_dp_recv)
+    proj_unit = unit(r.proj_made, r.proj_taken, r.proj_out, natural, r.proj_dp_send, r.proj_dp_recv)
+    conv_unit = unit(r.conv_made, r.conv_taken, r.conv_out, natural, r.conv_dp_send, r.conv_dp_recv)
 
     def halve(x, k, j):
         return remote(
@@ -366,7 +365,7 @@
         x.made[block_of(a, big), :] = value[:big]
         x.made[block_of(b, big), :] = value[big:]
 
-    def make_odd(u):
+    def make_odd(u, sent):
         x = bigs[u]
         if big % 128:
             left, right, h = sides[u]
@@ -382,10 +381,19 @@
             first = parts - 1 - 2 * t
             if big % 128 == 0:
                 make_pair(u, first, first - half)
-            halve(x, first, 0).start()
-            halve(x, first - half, 0).start()
+            if sent:
+                send_pair(x, t)
 
         loop(parts // 4, odd)
+
+    def send_pair(x, t):
+        first = parts - 1 - 2 * t
+        halve(x, first, 0).start()
+        halve(x, first - half, 0).start()
+
+    def send_pairs(x, start, stop):
+        for t in range(start, stop):
+            send_pair(x, t)
 
     def make_even(u):
         if big % 128 == 0:
@@ -424,9 +432,11 @@
         for k in range(parts - 1, 0, -2):
             halve(x, k, 0).start()
 
-    make_odd(0)
-    make_odd(1)
-    make_odd(2)
+    quarter_way = max(1, parts // 8)
+    make_odd(0, True)
+    make_odd(1, True)
+    make_odd(2, False)
+    send_pairs(in_a, 0, quarter_way)
 
     per = min(parts, max(1, 256 // share))
     channels = packed.shape[1]
@@ -514,7 +524,11 @@
         proj_columns(o).start()
 
     make_even(0)
+    settle_level(out_a, 1)
     make_even(1)
+    make_odd(3, False)
+    make_even(2)
+    make_even(3)
     for o in range(1, shards):
         columns(o).wait_recv()
     own_columns.wait()
@@ -535,11 +549,12 @@
     own_block = pltpu.make_async_copy(r.middle.at[d], r.back.at[d], r.own_sem.at[1])
     own_block.start()
 
-    settle_level(out_a, 1)
     settle_level(out_b, 1)
-    make_odd(3)
-    make_even(2)
-    make_even(3)
+    send_pairs(in_a, quarter_way, parts // 4)
+    send_pairs(in_b, 0, quarter_way)
+    for j in range(2, levels):
+        settle_level(out_a, j)
+    settle_level(in_a, 1)
 
     for o in range(1, shards):
         proj_columns(o).wait_recv()
@@ -549,14 +564,13 @@
     r.proj_made[...] = proj_total.astype(jnp.bfloat16)
 
     send_first(proj_unit)
-    for j in range(2, levels):
-        settle_level(out_a, j)
-        settle_level(out_b, j)
 
     for o in range(1, parts):
         give_back(o).wait_recv()
     own_block.wait()
     load_conv.wait()
+    for j in range(2, levels):
+        settle_level(out_b, j)
     returned = jnp.concatenate([r.back[e] for e in range(parts)], axis=0).T
     tile = min(256, frames)
 
@@ -571,22 +585,22 @@
     conv_term = jnp.dot(r.grad_pre[...], spare[...], preferred_element_type=jnp.float32)
     r.conv_made[...] = conv_term.T.astype(jnp.bfloat16)
     send_first(conv_unit)
-
+    send_pairs(in_b, quarter_way, parts // 4)
+
+    for j in range(2, levels):
+        settle_level(in_a, j)
     settle_level(proj_unit, 1)
-    settle_level(in_a, 1)
+    settle_level(in_b, 1)
     settle_level(conv_unit, 1)
     settle(out_a, 0)
     settle(out_b, 0)
     for j in range(2, levels):
+        settle_level(in_b, j)
         settle_level(proj_unit, j)
         settle_level(conv_unit, j)
-    settle_level(in_b, 1)
-    for j in range(2, levels):
-        settle_level(in_a, j)
-        settle_level(in_b, j)
+    settle(in_a, 0)
     settle(proj_unit, 0)
     settle(conv_unit, 0)
-    settle(in_a, 0)
     settle(in_b, 0)
 
     for o in range(1, parts):

time: 122 us -> 117 us (0.959)
  Pallas kernels: 121 us -> 116 us
    pallas_call x1, Pallas kernels: 119 us -> 114 us  [run_step(): pl.pallas_call(functools.partial(step_kernel, parts, shards, names), out_...]
where the time goes in v3:
time: 117 us
  Pallas kernels  116 us (99%)
    pallas_call x1, Pallas kernels, run_step(): pl.pallas_call(functools.partial(step_kernel, parts, shards, names), out_...  114 us

profile of v3, /device:TPU:1, one launch (start us, length us, event | category | flops | bytes accessed | tf_op | source)
XLA Modules:
  0.0 116.9 jit_solution(2893441694448890312)
XLA Ops:
  0.6 114.0 %step.1 = (f32[128,128]{1,0:T(8,128)}, f32[64,256]{1,0:T(8,128)}, f32[128,1024]{1,0:T(8,128)}, f32[128,1024]{1,0:T(8,128)}) custom-call(s32[1,2048]{1,0:T(1,128)} %bitcast.4, s32[1,2048]{1,0:T(1,128)} %bitcast.5, f32[1,512]{1,0:T(1,128)} %bitcast.7, f32[1,1024]{1,0:T(1,128)} %bitcast.6, bf16[2048,1024]{1,0:T(8,128)(2,1)} %refs_4_.1, ...), custom_call_target="tpu_custom_call" | custom-call | tf_op jit(solution)/shard_map/step/pallas_call | solution.py:712
  114.6 2.3 %hand_over.1 = (f32[128,128]{1,0:T(8,128)}, f32[64,256]{1,0:T(8,128)}, f32[128,1024]{1,0:T(8,128)}, f32[128,1024]{1,0:T(8,128)}) custom-call(f32[128,128]{1,0:T(8,128)} %get-tuple-element.8.refs_0_, f32[64,256]{1,0:T(8,128)} %get-tuple-element.9.refs_1_, f32[128,1024]{1,0:T(8,128)} %get-tuple-element.10.refs_2_, f32[128,1024]{1,0:T(8,128)} %get-tuple-element.11.refs_3_), custom_call_target="tpu_custom_call" | custom-call | tf_op jit(solution)/shard_map/hand_over/pallas_call | solution.py:731

commit v4 on v3

--- a/solution.py
+++ b/solution.py
@@ -230,18 +230,10 @@
     load_w_out.wait()
     load_cot.wait()
 
-    def grad_active(t):
-        span = block_of(t, rows)
-        value = jnp.dot(cot[span, :], w_out[...], preferred_element_type=jnp.float32)
-        spare[span, :] = (r.valid[span, :] * value).astype(jnp.bfloat16)
-        now = t // 2
-
-        @pl.when((lax.rem(t, 2) == 1) & (t > 1))
-        def _():
-            relay(now)
-            hand_on(now - 1)
-
-    loop(parts, grad_active)
+    lead = 2
+    for o in range(1, lead):
+        relay(o)
+        hand_on(o - 1)
     load_proj.wait()
     load_w_in.wait()
 
@@ -282,13 +274,13 @@
         s = source_of(o)
         span = block_of(s, rows)
 
-        @pl.when(o + half < parts)
+        @pl.when(o + lead < parts)
         def _():
-            relay(o + half)
-
-        @pl.when(o + half - 1 < parts)
+            relay(o + lead)
+
+        @pl.when(o + lead - 1 < parts)
         def _():
-            hand_on(o + half - 1)
+            hand_on(o + lead - 1)
 
         to_near(o, arrived.at[block_of(0, rows)]).wait_recv()
         for j in range(1, fars):
@@ -300,7 +292,8 @@
         normed, _ = normalize(hidden)
         r.hid_ln[span, :] = (normed * r.gain_block[...]).astype(jnp.bfloat16)
         lines = r.hid_ln[span, :]
-        keep_rows = r.valid[span, :]
+        masked = cot[span, :] * r.valid[span, :].astype(jnp.bfloat16)
+        cot[span, :] = masked
         units = w_in.shape[1]
         tile = min(256, units)
         for c in range(units // tile):
@@ -308,10 +301,9 @@
             upward = jnp.dot(lines, w_in[:, cols], preferred_element_type=jnp.float32)
             phi = 0.5 * (1.0 + lax.erf(upward * SQRT_HALF))
             slope = phi + upward * INV_SQRT_TWO_PI * jnp.exp(-0.5 * upward * upward)
-            r.active[span, cols] = (keep_rows * (upward * phi)).astype(jnp.bfloat16)
-            r.grad_up[span, cols] = (spare[span, cols].astype(jnp.float32) * slope).astype(
-                jnp.bfloat16
-            )
+            r.active[span, cols] = (upward * phi).astype(jnp.bfloat16)
+            grad_active = jnp.dot(masked, w_out[:, cols], preferred_element_type=jnp.float32)
+            r.grad_up[span, cols] = (grad_active * slope).astype(jnp.bfloat16)
         r.normed_part[span, :] = contract_cols(r.grad_up[span, :], w_in[...]).astype(
             jnp.bfloat16
         )
@@ -464,7 +456,7 @@
                 total = total + r.far_in[s, j].astype(jnp.float32)
             upstream.append(total)
         upstream = jnp.concatenate(upstream, axis=0)
-        direct = rows_of(r.valid) * rows_of(cot).astype(jnp.float32)
+        direct = rows_of(cot).astype(jnp.float32)
         grad_hidden = (
             direct + norm_back(upstream, hid_norm, hid_inv, r.gain_block[...])
         ).astype(jnp.bfloat16)
@@ -552,9 +544,9 @@
     settle_level(out_b, 1)
     send_pairs(in_a, quarter_way, parts // 4)
     send_pairs(in_b, 0, quarter_way)
+    settle_level(in_a, 1)
     for j in range(2, levels):
         settle_level(out_a, j)
-    settle_level(in_a, 1)
 
     for o in range(1, shards):
         proj_columns(o).wait_recv()

time: 117 us -> 118 us (level)
  no operation moved by 1% of the time
where the time goes in v4:
time: 118 us
  Pallas kernels  117 us (99%)
    pallas_call x1, Pallas kernels, run_step(): pl.pallas_call(functools.partial(step_kernel, parts, shards, names), out_...  115 us

profile of v4, /device:TPU:1, one launch (start us, length us, event | category | flops | bytes accessed | tf_op | source)
XLA Modules:
  0.0 117.7 jit_solution(9365330251474631839)
XLA Ops:
  0.6 114.8 %step.1 = (f32[128,128]{1,0:T(8,128)}, f32[64,256]{1,0:T(8,128)}, f32[128,1024]{1,0:T(8,128)}, f32[128,1024]{1,0:T(8,128)}) custom-call(s32[1,2048]{1,0:T(1,128)} %bitcast.4, s32[1,2048]{1,0:T(1,128)} %bitcast.5, f32[1,512]{1,0:T(1,128)} %bitcast.7, f32[1,1024]{1,0:T(1,128)} %bitcast.6, bf16[2048,1024]{1,0:T(8,128)(2,1)} %refs_4_.1, ...), custom_call_target="tpu_custom_call" | custom-call | tf_op jit(solution)/shard_map/step/pallas_call | solution.py:704
  115.4 2.3 %hand_over.1 = (f32[128,128]{1,0:T(8,128)}, f32[64,256]{1,0:T(8,128)}, f32[128,1024]{1,0:T(8,128)}, f32[128,1024]{1,0:T(8,128)}) custom-call(f32[128,128]{1,0:T(8,128)} %get-tuple-element.8.refs_0_, f32[64,256]{1,0:T(8,128)} %get-tuple-element.9.refs_1_, f32[128,1024]{1,0:T(8,128)} %get-tuple-element.10.refs_2_, f32[128,1024]{1,0:T(8,128)} %get-tuple-element.11.refs_3_), custom_call_target="tpu_custom_call" | custom-call | tf_op jit(solution)/shard_map/hand_over/pallas_call | solution.py:723
